TPU v7x, 128 devices: a whole 4x4x4 slice. The times are simulated.
128 devices in a mesh: seq: 32 (over x, z, core), tm: 4 (over y).
Axes of the slice: x: 4, y: 4, z: 4, core: 2. Of those that a mesh axis runs over, the one named last changes fastest.
Arguments:
- latent: bfloat16 [8, 16384], P(None, ('seq', 'tm')), may hold values from -6 to 6
- first_kernel: bfloat16 [3, 3, 3, 16, 512], replicated, may hold values from -0.3125 to 0.3125
- first_bias: float32 [512], replicated, may hold values from -3 to 3
- first_gain: float32 [512], replicated, may hold values from 0.1 to 1.9
- second_kernel: bfloat16 [3, 3, 3, 512, 256], replicated, may hold values from -0.0546875 to 0.0546875
- second_bias: float32 [256], replicated, may hold values from -3 to 3
- second_gain: float32 [256], replicated, may hold values from 0.1 to 1.9
- final_kernel: bfloat16 [3, 3, 3, 256, 128], replicated, may hold values from -0.078125 to 0.078125
- final_bias: float32 [128], replicated, may hold values from -2 to 2
Outputs:
- decoded: bfloat16 [8, 128, 128, 128], P('tm', 'seq')
All inputs are finite; a program needn't handle non-finite values.
Results may differ from a plain program's by a relative error of at most 0.0051.
Values may be sent and summed in bfloat16 or wider, within the bound.
A program may use at most 64 MiB of HBM per device.

v0:
```python
import jax
import jax.numpy as jnp
from jax import lax
from jax.sharding import PartitionSpec as P

RH = 1


def passed_along(array, axis, by):
    devices = lax.axis_size(axis)
    pairs = [(i, i + by) for i in range(devices) if 0 <= i + by < devices]
    return lax.ppermute(array, axis, pairs)


def padded_2(array, sides, width):
    for axis, dim in sides:
        devices, length = (lax.axis_size(axis), array.shape[dim])
        up = [(i, (i + 1) % devices) for i in range(devices - 1)]
        down = [(j, i) for i, j in up]
        last = lax.slice_in_dim(array, length - width, length, axis=dim)
        first = lax.slice_in_dim(array, 0, width, axis=dim)
        before = lax.ppermute(last, axis, up)
        after = lax.ppermute(first, axis, down)
        array = jnp.concatenate([before, array, after], axis=dim)
    return array


def conv_taps(padded, kernel, offset):
    frames = padded.shape[0] - 2
    height = padded.shape[1] - 2
    columns = padded.shape[2] - 2
    in_channels = padded.shape[3]
    out_channels = kernel.shape[4]
    summed = jnp.zeros((frames, height, columns, out_channels), jnp.float32)
    for time_tap in range(3):
        for row_tap in range(3):
            slab_rows = padded[time_tap : time_tap + frames, row_tap : row_tap + height]
            stacked = jnp.concatenate(
                [slab_rows[:, :, col_tap : col_tap + columns] for col_tap in range(3)], axis=3
            )
            matrix = kernel[time_tap, row_tap].reshape(3 * in_channels, out_channels)
            summed = summed + jnp.einsum(
                "abcd,de->abce", stacked, matrix, preferred_element_type=jnp.float32
            )
    return summed + offset


def activate(hidden, norm_gain):
    factor = lax.rsqrt(jnp.mean(hidden * hidden, axis=3, keepdims=True) + 1e-06)
    return jax.nn.silu(hidden * factor * norm_gain).astype(jnp.bfloat16)


def causal_frames(tensor, before):
    repeated = jnp.concatenate([tensor[:1], tensor[:1]], axis=0)
    at_start = lax.axis_index("tm") == 0
    return jnp.concatenate([jnp.where(at_start, repeated, before), tensor], axis=0)


def edge_rows(tensor, extended):
    top_row = jnp.where(lax.axis_index("seq") == 0, tensor[:, :1], extended[:, :1])
    bottom_row = jnp.where(
        lax.axis_index("seq") == lax.axis_size("seq") - 1, tensor[:, -1:], extended[:, -1:]
    )
    return jnp.concatenate([top_row, tensor, bottom_row], axis=1)


def double_size(tensor):
    return jnp.repeat(jnp.repeat(tensor, 2, axis=1), 2, axis=2)


def pad_columns(tensor):
    return jnp.pad(tensor, ((0, 0), (0, 0), (1, 1), (0, 0)), mode="edge")


def per_device(
    latent,
    first_kernel,
    first_bias,
    first_gain,
    second_kernel,
    second_bias,
    second_gain,
    final_kernel,
    final_bias,
):
    tm_count = lax.axis_size("tm")
    frame_count = latent.shape[0] // tm_count
    channels = first_kernel.shape[3]
    tokens = lax.all_to_all(latent, "tm", split_axis=0, concat_axis=1, tiled=True)
    latent_grid = tokens.reshape(frame_count, RH, -1, channels)
    before = passed_along(latent_grid, "tm", 1)
    with_time = causal_frames(latent_grid, before)
    beside = padded_2(with_time, (("seq", 1),), 1)
    padded = pad_columns(edge_rows(with_time, beside))
    first_act = activate(conv_taps(padded, first_kernel, first_bias), first_gain)
    before = passed_along(first_act, "tm", 1)
    with_time = causal_frames(first_act, before)
    beside = padded_2(with_time, (("seq", 1),), 1)
    widened = double_size(edge_rows(with_time, beside))
    hidden = conv_taps(pad_columns(widened[:, 1:-1]), second_kernel, second_bias)
    second_act = activate(hidden, second_gain)
    before = passed_along(second_act, "tm", 1)
    with_time = causal_frames(second_act, before)
    beside = padded_2(with_time, (("seq", 1),), 1)
    extended = edge_rows(with_time, beside)
    enlarged = double_size(extended)[:, 1:-1]
    decoded = conv_taps(pad_columns(enlarged), final_kernel, final_bias)
    return decoded.astype(jnp.bfloat16)


def solution(mesh):
    placed = (P(None, ("seq", "tm")), P(), P(), P(), P(), P(), P(), P(), P())
    return jax.shard_map(
        per_device,
        mesh=mesh,
        in_specs=placed,
        out_specs=P("tm", "seq", None, None),
        check_vma=False,
    )
```

profile of v0, /device:TPU:15, one launch (start us, length us, event | category | flops | bytes accessed | tf_op | source)
XLA Modules:
  0.0 94.5 jit_solution(6136264145459314241)
XLA Ops:
  0.0 4.3 %all-to-all-start = ((bf16[4,2,128]{2,1,0:T(2,128)(2,1)}), bf16[4,2,128]{2,1,0:T(2,128)(2,1)S(1)}, u32[]{:S(2)}, u32[]{:S(2)}) async-start(bf16[4,2,128]{2,1,0:T(2,128)(2,1)} %bitcast.215), calls=%async_computation | async-start | bytes 4096 | tf_op jit(solution)/shard_map/all_to_all | solution.py:89
  4.4 1.0 %fusion.257 = (bf16[1,1,3,16,512]{4,3,2,1,0:T(8,128)(2,1)S(1)}, bf16[1,1,3,16,512]{4,3,2,1,0:T(8,128)(2,1)S(1)}, bf16[1,1,3,16,512]{4,3,2,1,0:T(8,128)(2,1)S(1)}...) fusion(bf16[3,3,3,16,512]{4,3,2,1,0:T(8,128)(2,1)} %param.10), kind=kLoop, calls=%fused_computation.359 | loop fusion | bytes 884736 | tf_op jit(solution)/shard_map/slice | solution.py:41
  5.4 1.8 %all-to-all-done = bf16[4,2,128]{2,1,0:T(2,128)(2,1)S(1)} async-done(((bf16[4,2,128]{2,1,0:T(2,128)(2,1)}), bf16[4,2,128]{2,1,0:T(2,128)(2,1)S(1)}, u32[]{:S(2)}, u32[]{:S(2)}) %all-to-all-start) | async-done | bytes 2080 | tf_op jit(solution)/shard_map/all_to_all | solution.py:89
  7.3 2.2 %collective-permute-start = (bf16[2,1,32,16]{3,2,0,1:T(8,128)(2,1)S(1)}, bf16[2,1,32,16]{3,2,0,1:T(8,128)(2,1)S(1)}, u32[]{:S(2)}, u32[]{:S(2)}) collective-permute-start(bf16[2,1,32,16]{3,2,0,1:T(8,128)(2,1)S(1)} %reshape.105), channel_id=1, source_target_pairs={{0,1},{1,2},{2,3},{4,5},{5,6},{6,7},{8,9},{9,10},{10,11},{12,13},{... | collective-permute-start | bytes 6152 | tf_op jit(solution)/shard_map/ppermute | solution.py:12
  9.6 2.2 %collective-permute-done = bf16[2,1,32,16]{3,2,0,1:T(8,128)(2,1)S(1)} collective-permute-done((bf16[2,1,32,16]{3,2,0,1:T(8,128)(2,1)S(1)}, bf16[2,1,32,16]{3,2,0,1:T(8,128)(2,1)S(1)}, u32[]{:S(2)}, u32[]{:S(2)}) %collective-permute-start) | collective-permute-done | bytes 2080 | tf_op jit(solution)/shard_map/ppermute | solution.py:12
  11.8 5.2 %collective-permute-start.2 = (bf16[4,1,32,16]{3,2,0,1:T(8,128)(2,1)S(1)}, bf16[4,1,32,16]{3,2,0,1:T(8,128)(2,1)S(1)}, u32[]{:S(2)}, u32[]{:S(2)}) collective-permute-start(bf16[4,1,32,16]{3,2,0,1:T(8,128)(2,1)S(1)} %pad_maximum_fusion.14), channel_id=1, source_target_pairs={{4,0},{8,4},{12,8},{16,12},{20,16},{24,20},{28,24},{32,28},{36,32}... | collective-permute-start | bytes 12296 | tf_op jit(solution)/shard_map/ppermute | solution.py:23
  17.0 3.4 %collective-permute-start.1 = (bf16[4,1,32,16]{3,2,0,1:T(8,128)(2,1)S(1)}, bf16[4,1,32,16]{3,2,0,1:T(8,128)(2,1)S(1)}, u32[]{:S(2)}, u32[]{:S(2)}) collective-permute-start(bf16[4,1,32,16]{3,2,0,1:T(8,128)(2,1)S(1)} %pad_maximum_fusion.14), channel_id=1, source_target_pairs={{0,4},{4,8},{8,12},{12,16},{16,20},{20,24},{24,28},{28,32},{32,36}... | collective-permute-start | bytes 12296 | tf_op jit(solution)/shard_map/ppermute | solution.py:22
  20.4 1.0 %collective-permute-done.1 = bf16[4,1,32,16]{3,2,0,1:T(8,128)(2,1)S(1)} collective-permute-done((bf16[4,1,32,16]{3,2,0,1:T(8,128)(2,1)S(1)}, bf16[4,1,32,16]{3,2,0,1:T(8,128)(2,1)S(1)}, u32[]{:S(2)}, u32[]{:S(2)}) %collective-permute-start.1) | collective-permute-done | bytes 4128 | tf_op jit(solution)/shard_map/ppermute | solution.py:22
  23.9 2.2 %collective-permute-start.3 = (bf16[2,1,32,512]{3,2,0,1:T(8,128)(2,1)S(1)}, bf16[2,1,32,512]{3,2,0,1:T(8,128)(2,1)S(1)}, u32[]{:S(2)}, u32[]{:S(2)}) collective-permute-start(bf16[2,1,32,512]{3,2,0,1:T(8,128)(2,1)S(1)} %fusion.289), channel_id=1, source_target_pairs={{0,1},{1,2},{2,3},{4,5},{5,6},{6,7},{8,9},{9,10},{10,11},{12,13},{... | collective-permute-start | bytes 196616 | tf_op jit(solution)/shard_map/ppermute | solution.py:12
  26.1 2.8 %collective-permute-done.3 = bf16[2,1,32,512]{3,2,0,1:T(8,128)(2,1)S(1)} collective-permute-done((bf16[2,1,32,512]{3,2,0,1:T(8,128)(2,1)S(1)}, bf16[2,1,32,512]{3,2,0,1:T(8,128)(2,1)S(1)}, u32[]{:S(2)}, u32[]{:S(2)}) %collective-permute-start.3) | collective-permute-done | bytes 65568 | tf_op jit(solution)/shard_map/ppermute | solution.py:12
  28.9 7.1 %collective-permute-start.5 = (bf16[4,1,32,512]{3,2,0,1:T(8,128)(2,1)S(1)}, bf16[4,1,32,512]{3,2,0,1:T(8,128)(2,1)S(1)}, u32[]{:S(2)}, u32[]{:S(2)}) collective-permute-start(bf16[4,1,32,512]{3,2,0,1:T(8,128)(2,1)S(1)} %pad_maximum_fusion.13), channel_id=1, source_target_pairs={{4,0},{8,4},{12,8},{16,12},{20,16},{24,20},{28,24},{32,28},{36,32}... | collective-permute-start | bytes 393224 | tf_op jit(solution)/shard_map/ppermute | solution.py:23
  36.0 1.9 %collective-permute-start.4 = (bf16[4,1,32,512]{3,2,0,1:T(8,128)(2,1)S(1)}, bf16[4,1,32,512]{3,2,0,1:T(8,128)(2,1)S(1)}, u32[]{:S(2)}, u32[]{:S(2)}) collective-permute-start(bf16[4,1,32,512]{3,2,0,1:T(8,128)(2,1)S(1)} %pad_maximum_fusion.13), channel_id=1, source_target_pairs={{0,4},{4,8},{8,12},{12,16},{16,20},{20,24},{24,28},{28,32},{32,36}... | collective-permute-start | bytes 393224 | tf_op jit(solution)/shard_map/ppermute | solution.py:22
  38.0 5.9 %fusion.251 = (bf16[1,1,3,512,256]{4,3,2,1,0:T(8,128)(2,1)}, bf16[1,1,3,512,256]{4,3,2,1,0:T(8,128)(2,1)}, bf16[1,1,3,512,256]{4,3,2,1,0:T(8,128)(2,1)}, bf16[1,...) fusion(bf16[3,3,3,512,256]{4,3,2,1,0:T(8,128)(2,1)} %param.13), kind=kLoop, calls=%fused_computation.353 | loop fusion | bytes 14155776 | tf_op jit(solution)/shard_map/slice | solution.py:41
  44.1 1.1 %broadcast_in_dim.9 = bf16[4,6,32,2,512]{4,3,2,1,0:T(2,128)(2,1)S(1)} broadcast(bf16[4,6,32,512]{3,2,1,0:T(8,128)(2,1)S(1)} %bitcast.184), dimensions={0,1,2,4} | broadcast | bytes 2359296 | tf_op jit(solution)/shard_map/broadcast_in_dim | solution.py:68
  57.3 2.3 %collective-permute-start.6 = (bf16[2,2,64,256]{3,2,1,0:T(8,128)(2,1)S(1)}, bf16[2,2,64,256]{3,2,1,0:T(8,128)(2,1)S(1)}, u32[]{:S(2)}, u32[]{:S(2)}) collective-permute-start(bf16[2,2,64,256]{3,2,1,0:T(8,128)(2,1)S(1)} %multiply_convert_fusion), channel_id=1, source_target_pairs={{0,1},{1,2},{2,3},{4,5},{5,6},{6,7},{8,9},{9,10},{10,11},{12,13},{... | collective-permute-start | bytes 393224 | tf_op jit(solution)/shard_map/ppermute | solution.py:12
  59.7 4.2 %collective-permute-done.6 = bf16[2,2,64,256]{3,2,1,0:T(8,128)(2,1)S(1)} collective-permute-done((bf16[2,2,64,256]{3,2,1,0:T(8,128)(2,1)S(1)}, bf16[2,2,64,256]{3,2,1,0:T(8,128)(2,1)S(1)}, u32[]{:S(2)}, u32[]{:S(2)}) %collective-permute-start.6) | collective-permute-done | bytes 131104 | tf_op jit(solution)/shard_map/ppermute | solution.py:12
  63.9 2.0 %collective-permute-start.7 = (bf16[4,1,64,256]{3,2,1,0:T(8,128)(2,1)S(1)}, bf16[4,1,64,256]{3,2,1,0:T(8,128)(2,1)S(1)}, u32[]{:S(2)}, u32[]{:S(2)}) collective-permute-start(bf16[4,1,64,256]{3,2,1,0:T(8,128)(2,1)S(1)} %pad_maximum_fusion.12), channel_id=1, source_target_pairs={{0,4},{4,8},{8,12},{12,16},{16,20},{20,24},{24,28},{28,32},{32,36}... | collective-permute-start | bytes 393224 | tf_op jit(solution)/shard_map/ppermute | solution.py:22
  65.9 2.1 %collective-permute-done.7 = bf16[4,1,64,256]{3,2,1,0:T(8,128)(2,1)S(1)} collective-permute-done((bf16[4,1,64,256]{3,2,1,0:T(8,128)(2,1)S(1)}, bf16[4,1,64,256]{3,2,1,0:T(8,128)(2,1)S(1)}, u32[]{:S(2)}, u32[]{:S(2)}) %collective-permute-start.7) | collective-permute-done | bytes 131104 | tf_op jit(solution)/shard_map/ppermute | solution.py:22
  68.1 7.7 %collective-permute-start.8 = (bf16[4,1,64,256]{3,2,1,0:T(8,128)(2,1)S(1)}, bf16[4,1,64,256]{3,2,1,0:T(8,128)(2,1)S(1)}, u32[]{:S(2)}, u32[]{:S(2)}) collective-permute-start(bf16[4,1,64,256]{3,2,1,0:T(8,128)(2,1)S(1)} %get-tuple-element.6), channel_id=1, source_target_pairs={{4,0},{8,4},{12,8},{16,12},{20,16},{24,20},{28,24},{32,28},{36,32}... | collective-permute-start | bytes 393224 | tf_op jit(solution)/shard_map/ppermute | solution.py:23
  76.9 3.0 %broadcast_in_dim.22 = bf16[4,8,64,2,256]{4,3,2,1,0:T(2,128)(2,1)} broadcast(bf16[4,8,64,256]{3,2,1,0:T(8,128)(2,1)S(1)} %bitcast.183), dimensions={0,1,2,4} | broadcast | bytes 3145728 | tf_op jit(solution)/shard_map/broadcast_in_dim | solution.py:68
  79.9 2.7 %reshape.118 = bf16[4,8,128,256]{3,2,1,0:T(8,128)(2,1)S(1)} reshape(bf16[4,8,64,2,256]{4,3,2,1,0:T(2,128)(2,1)} %broadcast_in_dim.22) | data formatting | bytes 4194304 | tf_op jit(solution)/shard_map/reshape | solution.py:68
  83.4 2.4 %fusion.144 = (bf16[2,4,128,256]{3,2,1,0:T(8,128)(2,1)S(1)}, bf16[2,4,128,256]{3,2,1,0:T(8,128)(2,1)S(1)}, bf16[2,4,128,256]{3,2,1,0:T(8,128)(2,1)S(1)}, bf16[2,...) fusion(bf16[4,6,128,256]{3,2,1,0:T(8,128)(2,1)S(1)} %slice.793,, ...), kind=kLoop, calls=%fused_computation.204 | loop fusion | flops 8388608 | bytes 5779456 | tf_op jit(solution)/shard_map/jit(_pad)/concatenate | solution.py:72
  85.8 2.3 %fusion.136 = (bf16[2,4,128,256]{3,2,1,0:T(8,128)(2,1)S(1)}, bf16[2,4,128,256]{3,2,1,0:T(8,128)(2,1)S(1)}, bf16[2,4,128,256]{3,2,1,0:T(8,128)(2,1)S(1)}, bf16[2,...) fusion(bf16[4,6,128,256]{3,2,1,0:T(8,128)(2,1)S(1)} %slice.793,, ...), kind=kLoop, calls=%fused_computation.196 | loop fusion | flops 8388608 | bytes 5779456 | tf_op jit(solution)/shard_map/jit(_pad)/concatenate | solution.py:72
  93.2 1.3 %fusion.83 = bf16[2,4,128,128]{3,2,1,0:T(8,128)(2,1)} fusion(f32[2,4,128,128]{3,2,1,0:T(8,128)S(1)} %fusion.1, f32[2,4,128,128]{3,2,1,0:T(8,128)S(1)} %fusion.59, bf16[768,128,1,1]{1,0,3,2:T(8,128)(2,1)S(1)} %bitcast.194, bf16[2,4,128,256]{3,2,1,0:T(8,128)(2,1)S(1)} %get-tuple-element.44, bf16[2,4,128,256]{3,2,1,0:T(8,128)(2,1)S(1)} %get-tuple-element.16, ...), kind=kOutput, calls=%fused_computation.97 | convolution fusion | flops 206569472 | bytes 3080704 | tf_op jit(solution)/shard_map/abcd,de->abce/dot_general | solution.py:42
  (104 shorter events, 21.6 us)
Async XLA Ops:
  0.0 7.2 %all-to-all-start = ((bf16[4,2,128]{2,1,0:T(2,128)(2,1)}), bf16[4,2,128]{2,1,0:T(2,128)(2,1)S(1)}, u32[]{:S(2)}, u32[]{:S(2)}) async-start(bf16[4,2,128]{2,1,0:T(2,128)(2,1)} %bitcast.215), calls=%async_computation | async-start | bytes 4096 | tf_op jit(solution)/shard_map/all_to_all | solution.py:89
  7.3 4.5 %collective-permute-start = (bf16[2,1,32,16]{3,2,0,1:T(8,128)(2,1)S(1)}, bf16[2,1,32,16]{3,2,0,1:T(8,128)(2,1)S(1)}, u32[]{:S(2)}, u32[]{:S(2)}) collective-permute-start(bf16[2,1,32,16]{3,2,0,1:T(8,128)(2,1)S(1)} %reshape.105), channel_id=1, source_target_pairs={{0,1},{1,2},{2,3},{4,5},{5,6},{6,7},{8,9},{9,10},{10,11},{12,13},{... | collective-permute-start | bytes 6152 | tf_op jit(solution)/shard_map/ppermute | solution.py:12
  11.8 8.6 %collective-permute-start.2 = (bf16[4,1,32,16]{3,2,0,1:T(8,128)(2,1)S(1)}, bf16[4,1,32,16]{3,2,0,1:T(8,128)(2,1)S(1)}, u32[]{:S(2)}, u32[]{:S(2)}) collective-permute-start(bf16[4,1,32,16]{3,2,0,1:T(8,128)(2,1)S(1)} %pad_maximum_fusion.14), channel_id=1, source_target_pairs={{4,0},{8,4},{12,8},{16,12},{20,16},{24,20},{28,24},{32,28},{36,32}... | collective-permute-start | bytes 12296 | tf_op jit(solution)/shard_map/ppermute | solution.py:23
  17.0 4.5 %collective-permute-start.1 = (bf16[4,1,32,16]{3,2,0,1:T(8,128)(2,1)S(1)}, bf16[4,1,32,16]{3,2,0,1:T(8,128)(2,1)S(1)}, u32[]{:S(2)}, u32[]{:S(2)}) collective-permute-start(bf16[4,1,32,16]{3,2,0,1:T(8,128)(2,1)S(1)} %pad_maximum_fusion.14), channel_id=1, source_target_pairs={{0,4},{4,8},{8,12},{12,16},{16,20},{20,24},{24,28},{28,32},{32,36}... | collective-permute-start | bytes 12296 | tf_op jit(solution)/shard_map/ppermute | solution.py:22
  21.5 1.8 %copy-start.13 = (f32[512]{0:T(512)S(1)}, f32[512]{0:T(512)}, u32[]{:S(2)}) copy-start(f32[512]{0:T(512)} %param.11) | copy-start | bytes 6148
  21.6 2.0 %copy-start.12 = (f32[512]{0:T(512)S(1)}, f32[512]{0:T(512)}, u32[]{:S(2)}) copy-start(f32[512]{0:T(512)} %param.12) | copy-start | bytes 6148
  23.9 5.0 %collective-permute-start.3 = (bf16[2,1,32,512]{3,2,0,1:T(8,128)(2,1)S(1)}, bf16[2,1,32,512]{3,2,0,1:T(8,128)(2,1)S(1)}, u32[]{:S(2)}, u32[]{:S(2)}) collective-permute-start(bf16[2,1,32,512]{3,2,0,1:T(8,128)(2,1)S(1)} %fusion.289), channel_id=1, source_target_pairs={{0,1},{1,2},{2,3},{4,5},{5,6},{6,7},{8,9},{9,10},{10,11},{12,13},{... | collective-permute-start | bytes 196616 | tf_op jit(solution)/shard_map/ppermute | solution.py:12
  28.9 15.0 %collective-permute-start.5 = (bf16[4,1,32,512]{3,2,0,1:T(8,128)(2,1)S(1)}, bf16[4,1,32,512]{3,2,0,1:T(8,128)(2,1)S(1)}, u32[]{:S(2)}, u32[]{:S(2)}) collective-permute-start(bf16[4,1,32,512]{3,2,0,1:T(8,128)(2,1)S(1)} %pad_maximum_fusion.13), channel_id=1, source_target_pairs={{4,0},{8,4},{12,8},{16,12},{20,16},{24,20},{28,24},{32,28},{36,32}... | collective-permute-start | bytes 393224 | tf_op jit(solution)/shard_map/ppermute | solution.py:23
  36.0 7.8 %collective-permute-start.4 = (bf16[4,1,32,512]{3,2,0,1:T(8,128)(2,1)S(1)}, bf16[4,1,32,512]{3,2,0,1:T(8,128)(2,1)S(1)}, u32[]{:S(2)}, u32[]{:S(2)}) collective-permute-start(bf16[4,1,32,512]{3,2,0,1:T(8,128)(2,1)S(1)} %pad_maximum_fusion.13), channel_id=1, source_target_pairs={{0,4},{4,8},{8,12},{12,16},{16,20},{20,24},{24,28},{28,32},{32,36}... | collective-permute-start | bytes 393224 | tf_op jit(solution)/shard_map/ppermute | solution.py:22
  46.9 1.1 %copy-start.9 = (bf16[1,1,3,512,256]{4,3,2,1,0:T(8,128)(2,1)S(1)}, bf16[1,1,3,512,256]{4,3,2,1,0:T(8,128)(2,1)}, u32[]{:S(2)}) copy-start(bf16[1,1,3,512,256]{4,3,2,1,0:T(8,128)(2,1)} %get-tuple-element.14) | copy-start | bytes 2359300
  47.4 1.2 %copy-start.8 = (bf16[1,1,3,512,256]{4,3,2,1,0:T(8,128)(2,1)S(1)}, bf16[1,1,3,512,256]{4,3,2,1,0:T(8,128)(2,1)}, u32[]{:S(2)}) copy-start(bf16[1,1,3,512,256]{4,3,2,1,0:T(8,128)(2,1)} %get-tuple-element.13) | copy-start | bytes 2359300
  48.6 1.1 %copy-start.7 = (bf16[1,1,3,512,256]{4,3,2,1,0:T(8,128)(2,1)S(1)}, bf16[1,1,3,512,256]{4,3,2,1,0:T(8,128)(2,1)}, u32[]{:S(2)}) copy-start(bf16[1,1,3,512,256]{4,3,2,1,0:T(8,128)(2,1)} %get-tuple-element.12) | copy-start | bytes 2359300
  49.7 1.1 %copy-start.6 = (bf16[1,1,3,512,256]{4,3,2,1,0:T(8,128)(2,1)S(1)}, bf16[1,1,3,512,256]{4,3,2,1,0:T(8,128)(2,1)}, u32[]{:S(2)}) copy-start(bf16[1,1,3,512,256]{4,3,2,1,0:T(8,128)(2,1)} %get-tuple-element.11) | copy-start | bytes 2359300
  50.8 1.1 %copy-start.5 = (bf16[1,1,3,512,256]{4,3,2,1,0:T(8,128)(2,1)S(1)}, bf16[1,1,3,512,256]{4,3,2,1,0:T(8,128)(2,1)}, u32[]{:S(2)}) copy-start(bf16[1,1,3,512,256]{4,3,2,1,0:T(8,128)(2,1)} %get-tuple-element.10) | copy-start | bytes 2359300
  52.0 1.1 %copy-start.4 = (bf16[1,1,3,512,256]{4,3,2,1,0:T(8,128)(2,1)S(1)}, bf16[1,1,3,512,256]{4,3,2,1,0:T(8,128)(2,1)}, u32[]{:S(2)}) copy-start(bf16[1,1,3,512,256]{4,3,2,1,0:T(8,128)(2,1)} %get-tuple-element.9) | copy-start | bytes 2359300
  53.1 1.1 %copy-start.3 = (bf16[1,1,3,512,256]{4,3,2,1,0:T(8,128)(2,1)S(1)}, bf16[1,1,3,512,256]{4,3,2,1,0:T(8,128)(2,1)}, u32[]{:S(2)}) copy-start(bf16[1,1,3,512,256]{4,3,2,1,0:T(8,128)(2,1)} %get-tuple-element.8) | copy-start | bytes 2359300
  54.2 1.1 %copy-start.2 = (bf16[1,1,3,512,256]{4,3,2,1,0:T(8,128)(2,1)S(1)}, bf16[1,1,3,512,256]{4,3,2,1,0:T(8,128)(2,1)}, u32[]{:S(2)}) copy-start(bf16[1,1,3,512,256]{4,3,2,1,0:T(8,128)(2,1)} %get-tuple-element.15) | copy-start | bytes 2359300
  55.4 1.1 %copy-start.1 = (bf16[1,1,3,512,256]{4,3,2,1,0:T(8,128)(2,1)S(1)}, bf16[1,1,3,512,256]{4,3,2,1,0:T(8,128)(2,1)}, u32[]{:S(2)}) copy-start(bf16[1,1,3,512,256]{4,3,2,1,0:T(8,128)(2,1)} %get-tuple-element.7) | copy-start | bytes 2359300
  55.4 1.1 %copy-start.15 = (f32[256]{0:T(256)S(1)}, f32[256]{0:T(256)}, u32[]{:S(2)}) copy-start(f32[256]{0:T(256)} %param.14) | copy-start | bytes 3076
  57.0 18.9 %copy-start = (bf16[3,3,3,256,128]{4,3,2,1,0:T(8,128)(2,1)S(1)}, bf16[3,3,3,256,128]{4,3,2,1,0:T(8,128)(2,1)}, u32[]{:S(2)}) copy-start(bf16[3,3,3,256,128]{4,3,2,1,0:T(8,128)(2,1)} %param.16) | copy-start | bytes 5308420
  57.3 6.5 %collective-permute-start.6 = (bf16[2,2,64,256]{3,2,1,0:T(8,128)(2,1)S(1)}, bf16[2,2,64,256]{3,2,1,0:T(8,128)(2,1)S(1)}, u32[]{:S(2)}, u32[]{:S(2)}) collective-permute-start(bf16[2,2,64,256]{3,2,1,0:T(8,128)(2,1)S(1)} %multiply_convert_fusion), channel_id=1, source_target_pairs={{0,1},{1,2},{2,3},{4,5},{5,6},{6,7},{8,9},{9,10},{10,11},{12,13},{... | collective-permute-start | bytes 393224 | tf_op jit(solution)/shard_map/ppermute | solution.py:12
  63.9 4.2 %collective-permute-start.7 = (bf16[4,1,64,256]{3,2,1,0:T(8,128)(2,1)S(1)}, bf16[4,1,64,256]{3,2,1,0:T(8,128)(2,1)S(1)}, u32[]{:S(2)}, u32[]{:S(2)}) collective-permute-start(bf16[4,1,64,256]{3,2,1,0:T(8,128)(2,1)S(1)} %pad_maximum_fusion.12), channel_id=1, source_target_pairs={{0,4},{4,8},{8,12},{12,16},{16,20},{20,24},{24,28},{28,32},{32,36}... | collective-permute-start | bytes 393224 | tf_op jit(solution)/shard_map/ppermute | solution.py:22
  68.1 8.6 %collective-permute-start.8 = (bf16[4,1,64,256]{3,2,1,0:T(8,128)(2,1)S(1)}, bf16[4,1,64,256]{3,2,1,0:T(8,128)(2,1)S(1)}, u32[]{:S(2)}, u32[]{:S(2)}) collective-permute-start(bf16[4,1,64,256]{3,2,1,0:T(8,128)(2,1)S(1)} %get-tuple-element.6), channel_id=1, source_target_pairs={{4,0},{8,4},{12,8},{16,12},{20,16},{24,20},{28,24},{32,28},{36,32}... | collective-permute-start | bytes 393224 | tf_op jit(solution)/shard_map/ppermute | solution.py:23
  85.8 2.3 %copy-start.11 = (bf16[1,1,3,256,128]{4,3,2,1,0:T(8,128)(2,1)S(1)}, bf16[1,1,3,256,128]{4,3,2,1,0:T(8,128)(2,1)}, u32[]{:S(2)}) copy-start(bf16[1,1,3,256,128]{4,3,2,1,0:T(8,128)(2,1)} %get-tuple-element.35) | copy-start | bytes 589828
  (3 other events, 2.3 us)
where the time goes:
time: 96.4 us; the launch traced here: 94.5 us
  starting transfers between devices  38.4 us (40%)
  local copies, waits for them, and re-layouts  23.4 us (24%)
  waiting for transfers between devices  14.1 us (15%)
  matrix products  11.5 us (12%)
  other arithmetic  6.45 us (7%)
    ppermute x3, starting transfers between devices, padded_2(): after = lax.ppermute(first, axis, down)  20 us
    dot_general x27, matrix products, conv_taps(): jnp.einsum('abcd,de->abce', stacked, matrix, preferred_element_type=jnp.f...  11.5 us
    ppermute x3, waiting for transfers between devices, passed_along(): return lax.ppermute(array, axis, pairs)  9.16 us
    slice x3, local copies, waits for them, and re-layouts, conv_taps(): matrix = kernel[time_tap, row_tap].reshape(3 * in_channels, out_channels)  7.8 us
    ppermute x3, starting transfers between devices, padded_2(): before = lax.ppermute(last, axis, up)  7.4 us
    ppermute x3, starting transfers between devices, passed_along(): return lax.ppermute(array, axis, pairs)  6.69 us
    unnamed x34, local copies, waits for them, and re-layouts  6.49 us
    concatenate x5, other arithmetic, pad_columns(): return jnp.pad(tensor, ((0, 0), (0, 0), (1, 1), (0, 0)), mode='edge')  5.78 us
  transfers between devices with their start and end apart: 10, of which 6 were waited for; matrix products, arithmetic and copies ran while one was open for 8% of the time, Pallas kernels for 0%

commit v1 on v0

v1 whole, which is shorter than its diff:
```python
import functools

import jax
import jax.numpy as jnp
from jax import lax
from jax.experimental import pallas as pl
from jax.experimental.pallas import tpu as pltpu
from jax.sharding import PartitionSpec as P

MESH = pl.DeviceIdType.MESH
F32 = jnp.float32
BF16 = jnp.bfloat16

SEQ = 32
TM = 4
W = 32
C1, C2, C3 = 512, 256, 128
EPS = 1e-06

CORNERS = ((0, 0), (0, 2), (2, 0), (2, 2))
OTHERS = ((0, 1), (1, 0), (1, 1), (1, 2), (2, 1))


def gather_kernel(x_ref, lat_ref, send_sem, recv_sem, own_sem):
    s, t = lax.axis_index("seq"), lax.axis_index("tm")
    peers = [(d, e) for d in (0, 1, -1, 2, -2) for e in range(TM) if (d, e) != (0, 0)]

    def where(d, e):
        return (lax.rem(s + (d + SEQ), SEQ), lax.rem(t + e, TM))

    barrier = pltpu.get_barrier_semaphore()
    for d, e in peers:
        pl.semaphore_signal(barrier, inc=1, device_id=where(d, e), device_id_type=MESH)
    own = pltpu.make_async_copy(x_ref, lat_ref.at[2, t], own_sem)
    own.start()
    pl.semaphore_wait(barrier, len(peers))
    copies = []
    for n, (d, e) in enumerate(peers):
        slot = 2 - d
        copy = pltpu.make_async_remote_copy(
            src_ref=x_ref,
            dst_ref=lat_ref.at[slot, t],
            send_sem=send_sem.at[n],
            recv_sem=recv_sem.at[slot, t],
            device_id=where(d, e),
            device_id_type=MESH,
        )
        copy.start()
        copies.append(copy)
    own.wait()
    for d, e in peers:
        frm = lax.rem(t + e, TM)
        pltpu.make_async_remote_copy(
            src_ref=x_ref,
            dst_ref=lat_ref.at[2 + d, frm],
            send_sem=send_sem.at[0],
            recv_sem=recv_sem.at[2 + d, frm],
            device_id=where(d, e),
            device_id_type=MESH,
        ).wait_recv()
    for copy in copies:
        copy.wait_send()


def gather_rows(latent):
    return pl.pallas_call(
        gather_kernel,
        out_shape=jax.ShapeDtypeStruct((5, TM, 8, 128), BF16),
        in_specs=[pl.BlockSpec(memory_space=pltpu.VMEM)],
        out_specs=pl.BlockSpec(memory_space=pltpu.VMEM),
        scratch_shapes=[
            pltpu.SemaphoreType.DMA((19,)),
            pltpu.SemaphoreType.DMA((5, TM)),
            pltpu.SemaphoreType.DMA,
        ],
        compiler_params=pltpu.CompilerParams(collective_id=0, has_side_effects=True),
        name="gather_rows",
    )(latent)


def silu_normed(hidden, gain):
    factor = lax.rsqrt(jnp.mean(hidden * hidden, axis=1, keepdims=True) + EPS)
    v = hidden * factor * gain
    half = 0.5 * v
    return (half + half * jnp.tanh(half)).astype(BF16)


def patches(lat_ref, pat_ref, s, t):
    late = 6 - 2 * t
    sub = lax.broadcasted_iota(jnp.int32, (8, 128), 0)
    lane = lax.broadcasted_iota(jnp.int32, (8, 128), 1)
    turned = []
    for q in range(5):
        row = jnp.clip(s - 2 + q, 0, SEQ - 1) - s + 2
        blocks = []
        for b in range(TM):
            x = lat_ref[row, b].astype(F32)
            moved = pltpu.roll(x, late, 0)
            x = jnp.where(sub < late, jnp.broadcast_to(x[0:1], (8, 128)), moved)
            blocks.append([pltpu.roll(x, (128 - 16 * (m - 1)) % 128, 1) for m in range(8)])
        turned.append(blocks)

    def piece(q, c, up):
        b, m = c // 8, c % 8
        k = (m + 4) % 8 if up else m
        base = 64 if up else 0
        own = turned[q][b][k]
        if m == 0:
            other = turned[q][b - 1][k] if b else turned[q][0][(k + 1) % 8]
            own = jnp.where(lane < base + 16, other, own)
        if m == 7:
            other = turned[q][b + 1][k] if b < 3 else turned[q][3][(k + 7) % 8]
            own = jnp.where(lane >= base + 32, other, own)
        return own

    for q in range(5):
        for c in range(W):
            low = piece(q, c, False)
            if q < 4:
                high = jnp.where((lane >= 64) & (lane < 112), piece(q + 1, c, True), 0.0)
            else:
                high = jnp.zeros((8, 128), F32)
            pat_ref[q, pl.ds(c, 8, stride=W), :] = jnp.where(lane < 48, low, high)


def sums(taps):
    r12 = [taps[1, k] + taps[2, k] for k in range(3)]
    r01 = [taps[0, k] + taps[1, k] for k in range(3)]
    k0 = [taps[0, k] for k in range(3)]
    k2 = [taps[2, k] for k in range(3)]
    total = lambda r: r[0] + r[1] + r[2]
    return {
        (0, 0, 1): total(k0),
        (0, 1, 0): r12[0],
        (0, 1, 1): total(r12),
        (0, 1, 2): r12[2],
        (1, 0, 0): r01[0],
        (1, 0, 1): total(r01),
        (1, 0, 2): r01[2],
        (1, 1, 1): total(k2),
    }


def corner_place(j, k):
    return (0, 0, k) if j == 0 else (1, 1, k)


def decode_kernel(
    lat_ref, w1_hbm, b1_ref, g1_ref, w2_hbm, b2_ref, g2_ref, w3_hbm, b3_ref,
    out_ref,
    w1, w2c, w2r, w3c, w3r, pat, x1, x2, o32, sem1, sem2, sem3,
):
    s, t = lax.axis_index("seq"), lax.axis_index("tm")

    copies1, copies2, copies3 = [], [[], [], []], []
    for i in range(3):
        for j in range(3):
            start = 256 * i + 64 * j
            copies1.append(
                pltpu.make_async_copy(w1_hbm.at[i, j], w1.at[pl.ds(start, 48), :], sem1.at[i, j])
            )
    for i in range(3):
        for j, k in CORNERS + OTHERS:
            if (j, k) in CORNERS:
                rp, u, b = corner_place(j, k)
                d2 = w2c.at[rp, b, u, i]
                d3 = w3c.at[rp, u, i, :, pl.ds(C3 * b, C3)]
            else:
                n = OTHERS.index((j, k))
                d2, d3 = w2r.at[i, n], w3r.at[i, n]
            copies2[i].append(pltpu.make_async_copy(w2_hbm.at[i, j, k], d2, sem2.at[i, j, k]))
            copies3.append(pltpu.make_async_copy(w3_hbm.at[i, j, k], d3, sem3.at[i, j, k]))
    zeros = jnp.zeros((16, C1), BF16)
    for i in range(3):
        for start in (48, 112, 176, 192, 208, 224, 240):
            w1[256 * i + start : 256 * i + start + 16, :] = zeros
    for copy in copies1 + copies2[0] + copies2[1] + copies2[2] + copies3:
        copy.start()

    patches(lat_ref, pat, s, t)
    lhs = []
    for r in range(3):
        q = jnp.clip(s - 1 + r, 0, SEQ - 1) - s + 1
        cols = []
        for i in range(3):
            for two in (0, 2):
                cols.append(pat[q + two, 32 * i : 32 * i + 192, :].astype(BF16))
        lhs.append(jnp.concatenate(cols, axis=1))
    lhs = jnp.concatenate(lhs, axis=0)
    for copy in copies1:
        copy.wait()
    hidden = jnp.dot(lhs, w1[...], preferred_element_type=F32) + b1_ref[...]
    act = silu_normed(hidden, g1_ref[...])
    for r in range(3):
        x1[r] = act[192 * r : 192 * r + 192]

    for i in range(3):
        for copy in copies2[i]:
            copy.wait()

        @pl.loop(0, C1 // 32)
        def _(n):
            rows = pl.ds(pl.multiple_of(32 * n, 32), 32)
            taps = {}
            for j, k in CORNERS:
                rp, u, b = corner_place(j, k)
                taps[j, k] = w2c[rp, b, u, i, rows, :].astype(F32)
            for m, (j, k) in enumerate(OTHERS):
                taps[j, k] = w2r[i, m, rows, :].astype(F32)
            for (rp, u, b), v in sums(taps).items():
                w2c[rp, b, u, i, rows, :] = v.astype(BF16)

    lhs = jnp.concatenate(
        [
            x1[u : u + 2, 32 * i : 32 * i + 128, :].reshape(256, C1)
            for u in range(2)
            for i in range(3)
        ],
        axis=1,
    )
    col = lax.broadcasted_iota(jnp.int32, (256, 1), 0) % W
    for rp in range(2):
        q0, qk, q2 = [
            jnp.dot(lhs, w2c[rp, b].reshape(6 * C1, C2), preferred_element_type=F32)
            for b in range(3)
        ]
        qk = qk + b2_ref[...]
        even = qk + jnp.where(col == 0, 0.0, pltpu.roll(q0, 1, 0) - q0)
        odd = qk + jnp.where(col == W - 1, 0.0, pltpu.roll(q2, 255, 0) - q2)
        for p, value in enumerate((even, odd)):
            act = silu_normed(value, g2_ref[...])
            for row in range(2):
                slot = 2 * row + 1 - rp
                for f in range(4):
                    part = act[128 * row + 32 * f : 128 * row + 32 * f + 32]
                    x2[slot, 64 * f + 32 * p : 64 * f + 32 * p + 32, :] = part

    for copy in copies3:
        copy.wait()

    @pl.loop(0, C2 // 32)
    def _(n):
        rows = pl.ds(pl.multiple_of(32 * n, 32), 32)
        for i in range(3):
            taps = {}
            for j, k in CORNERS:
                rp, u, b = corner_place(j, k)
                taps[j, k] = w3c[rp, u, i, rows, C3 * b : C3 * b + C3].astype(F32)
            for m, (j, k) in enumerate(OTHERS):
                taps[j, k] = w3r[i, m, rows, :].astype(F32)
            for (rp, u, b), v in sums(taps).items():
                w3c[rp, u, i, rows, C3 * b : C3 * b + C3] = v.astype(BF16)

    slots = [jnp.where(s == 0, 1, 0), 1, 2, jnp.where(s == SEQ - 1, 2, 3)]
    col = lax.broadcasted_iota(jnp.int32, (32, 1), 0)
    for rp in range(2):
        lhs = jnp.concatenate(
            [
                jnp.concatenate(
                    [x2[slots[rp + u + row], 64 * i : 64 * i + 128, :] for row in range(2)],
                    axis=0,
                )
                for u in range(2)
                for i in range(3)
            ],
            axis=1,
        )
        res = jnp.dot(lhs, w3c[rp].reshape(6 * C2, 3 * C3), preferred_element_type=F32)
        for row in range(2):
            for f in range(2):
                base = 128 * row + 64 * f
                (e0, ek, e2), (o0, ok, o2) = [
                    [
                        res[base + 32 * p : base + 32 * p + 32, C3 * b : C3 * b + C3]
                        for b in range(3)
                    ]
                    for p in range(2)
                ]
                ek = ek + b3_ref[...]
                ok = ok + b3_ref[...]
                values = (
                    ek + jnp.where(col == 0, 0.0, pltpu.roll(o0, 1, 0) - e0),
                    ek + (o2 - e2),
                    ok + (e0 - o0),
                    ok + jnp.where(col == W - 1, 0.0, pltpu.roll(e2, 31, 0) - o2),
                )
                for n, value in enumerate(values):
                    o32[f, 2 * row + rp, pl.ds(n, W, stride=4), :] = value
    out_ref[...] = o32[...].astype(BF16)


def decode(rows, w1, b1, g1, w2, b2, g2, w3, b3):
    vmem = pl.BlockSpec(memory_space=pltpu.VMEM)
    hbm = pl.BlockSpec(memory_space=pltpu.HBM)
    return pl.pallas_call(
        decode_kernel,
        out_shape=jax.ShapeDtypeStruct((2, 4, 128, C3), BF16),
        in_specs=[vmem, hbm, vmem, vmem, hbm, vmem, vmem, hbm, vmem],
        out_specs=vmem,
        scratch_shapes=[
            pltpu.VMEM((768, C1), BF16),
            pltpu.VMEM((2, 3, 2, 3, C1, C2), BF16),
            pltpu.VMEM((3, 5, C1, C2), BF16),
            pltpu.VMEM((2, 2, 3, C2, 3 * C3), BF16),
            pltpu.VMEM((3, 5, C2, C3), BF16),
            pltpu.VMEM((5, 8 * W, 128), F32),
            pltpu.VMEM((3, 6 * W, C1), BF16),
            pltpu.VMEM((4, 4 * 64, C2), BF16),
            pltpu.VMEM((2, 4, 128, C3), F32),
            pltpu.SemaphoreType.DMA((3, 3)),
            pltpu.SemaphoreType.DMA((3, 3, 3)),
            pltpu.SemaphoreType.DMA((3, 3, 3)),
        ],
        compiler_params=pltpu.CompilerParams(vmem_limit_bytes=56 << 20),
        name="decode",
    )(rows, w1, b1, g1, w2, b2, g2, w3, b3)


def per_device(latent, w1, b1, g1, w2, b2, g2, w3, b3):
    rows = gather_rows(latent)
    line = lambda v: v.reshape(1, -1)
    return decode(
        rows, w1.reshape(3, 3, 48, C1), line(b1), line(g1), w2, line(b2), line(g2), w3, line(b3)
    )


def solution(mesh):
    placed = (P(None, ("seq", "tm")), P(), P(), P(), P(), P(), P(), P(), P())
    return jax.shard_map(
        per_device,
        mesh=mesh,
        in_specs=placed,
        out_specs=P("tm", "seq", None, None),
        check_vma=False,
    )
```

time: 96.4 us -> 27.3 us (0.28)
  the two profiles are of different devices: /device:TPU:15 before, /device:TPU:1 now
where the time goes in v1:
time: 27.3 us; the launch traced here: 27.2 us
  Pallas kernels  27.2 us (100%)
    pallas_call x1, Pallas kernels, gather_rows(): pl.pallas_call(gather_kernel, out_shape=jax.ShapeDtypeStruct((5, TM, 8, 1...  14.6 us
    pallas_call x1, Pallas kernels, decode(): pl.pallas_call(decode_kernel, out_shape=jax.ShapeDtypeStruct((2, 4, 128,...  12.6 us

profile of v1, /device:TPU:1, one launch (start us, length us, event | category | flops | bytes accessed | tf_op | source)
XLA Modules:
  0.0 27.2 jit_solution(2038386041201829160)
XLA Ops:
  0.0 14.6 %gather_rows.1.lat_ref = bf16[5,4,8,128]{3,2,1,0:T(8,128)(2,1)} custom-call(bf16[8,128]{1,0:T(8,128)(2,1)} %x_ref.1), custom_call_target="tpu_custom_call" | custom-call | tf_op jit(solution)/shard_map/gather_rows/pallas_call | solution.py:66
  14.6 12.6 %decode.1 = bf16[2,4,128,128]{3,2,1,0:T(8,128)(2,1)} custom-call(bf16[5,4,8,128]{3,2,1,0:T(8,128)(2,1)} %gather_rows.1.lat_ref, bf16[3,3,48,512]{3,2,1,0:T(8,128)(2,1)} %bitcast.6, f32[1,512]{1,0:T(1,128)} %bitcast.7, f32[1,512]{1,0:T(1,128)} %bitcast.8, bf16[3,3,3,512,256]{4,3,2,1,0:T(8,128)(2,1)} %w2_hbm.1, f32[1,256]{1,0:T(1,128)} %bitcast.9, ...), custom_call_target="tpu_custom_call" | custom-call | tf_op jit(solution)/shard_map/decode/pallas_call | solution.py:295

commit v2 on v1

v2 whole, which is shorter than its diff:
```python
import jax
import jax.numpy as jnp
from jax import lax
from jax.experimental import pallas as pl
from jax.experimental.pallas import tpu as pltpu
from jax.sharding import PartitionSpec as P

MESH = pl.DeviceIdType.MESH
F32 = jnp.float32
BF16 = jnp.bfloat16

SEQ = 32
TM = 4
W = 32
C1, C2, C3 = 512, 256, 128
EPS = 1e-06

RAW = {(0, 0, 0): (0, 0), (0, 0, 2): (0, 2), (1, 1, 0): (2, 0), (1, 1, 2): (2, 2)}
SUMS = ((0, 0, 1), (0, 1, 0), (0, 1, 1), (0, 1, 2), (1, 0, 0), (1, 0, 1), (1, 0, 2), (1, 1, 1))
PEERS = tuple(
    (d, e) for d, e in (
        (2, 2), (-2, 2), (1, 2), (-1, 2), (2, 1), (2, 3), (-2, 1), (-2, 3), (0, 2), (1, 1), (1, 3),
        (-1, 1), (-1, 3), (2, 0), (-2, 0), (0, 1), (0, 3), (1, 0), (-1, 0),
    )
)


def silu_normed(hidden, gain):
    factor = lax.rsqrt(jnp.mean(hidden * hidden, axis=1, keepdims=True) + EPS)
    v = hidden * factor * gain
    half = 0.5 * v
    return (half + half * jnp.tanh(half)).astype(BF16)


def patches(lat_ref, pat_ref, s, t):
    late = 6 - 2 * t
    sub = lax.broadcasted_iota(jnp.int32, (8, 128), 0)
    lane = lax.broadcasted_iota(jnp.int32, (8, 128), 1)
    turned = []
    for q in range(5):
        row = jnp.clip(s - 2 + q, 0, SEQ - 1) - s + 2
        blocks = []
        for b in range(TM):
            x = lat_ref[row * TM + b].astype(F32)
            moved = pltpu.roll(x, late, 0)
            x = jnp.where(sub < late, jnp.broadcast_to(x[0:1], (8, 128)), moved)
            blocks.append([pltpu.roll(x, (128 - 16 * (m - 1)) % 128, 1) for m in range(8)])
        turned.append(blocks)

    def piece(q, c, up):
        b, m = c // 8, c % 8
        k = (m + 4) % 8 if up else m
        base = 64 if up else 0
        own = turned[q][b][k]
        if m == 0:
            other = turned[q][b - 1][k] if b else turned[q][0][(k + 1) % 8]
            own = jnp.where(lane < base + 16, other, own)
        if m == 7:
            other = turned[q][b + 1][k] if b < 3 else turned[q][3][(k + 7) % 8]
            own = jnp.where(lane >= base + 32, other, own)
        return own

    for q in range(5):
        for c in range(W):
            low = piece(q, c, False)
            if q < 4:
                high = jnp.where((lane >= 64) & (lane < 112), piece(q + 1, c, True), 0.0)
            else:
                high = jnp.zeros((8, 128), F32)
            pat_ref[q, pl.ds(c, 8, stride=W), :] = jnp.where(lane < 48, low, high)


def sums(taps):
    r12 = [taps[1, k] + taps[2, k] for k in range(3)]
    r01 = [taps[0, k] + taps[1, k] for k in range(3)]
    k0 = [taps[0, k] for k in range(3)]
    k2 = [taps[2, k] for k in range(3)]
    total = lambda r: r[0] + r[1] + r[2]
    return (total(k0), r12[0], total(r12), r12[2], r01[0], total(r01), r01[2], total(k2))


def add_taps(raw, summed, i, rows):
    taps = {(j, k): raw[i, j, k, rows, :].astype(F32) for j in range(3) for k in range(3)}
    for n, value in enumerate(sums(taps)):
        summed[i, n, rows, :] = value.astype(BF16)


def tap_matrix(raw, summed, rp, b):
    parts = []
    for u in range(2):
        for i in range(3):
            if (rp, u, b) in RAW:
                j, k = RAW[rp, u, b]
                parts.append(raw[i, j, k])
            else:
                parts.append(summed[i, SUMS.index((rp, u, b))])
    return jnp.concatenate(parts, axis=0)


def kernel(
    x_ref, w1_hbm, b1_ref, g1_ref, w2_hbm, b2_ref, g2_ref, w3_hbm, b3_ref,
    out_ref,
    lat, w1, w2, w2s, w3, w3s, pat, x1, x2, o32, send_sem, recv_sem, sem1, sem2, sem3,
):
    s, t = lax.axis_index("seq"), lax.axis_index("tm")

    def away(d, e):
        return (lax.rem(s + (d + SEQ), SEQ), lax.rem(t + e, TM))

    barrier = pltpu.get_barrier_semaphore()
    for d, e in PEERS:
        pl.semaphore_signal(barrier, inc=1, device_id=away(d, e), device_id_type=MESH)

    copies2 = [pltpu.make_async_copy(w2_hbm.at[i], w2.at[i], sem2.at[i]) for i in range(3)]
    copy1 = pltpu.make_async_copy(
        w1_hbm, w1.at[:, pl.ds(0, 3), pl.ds(0, 48), :], sem1
    )
    copy3 = pltpu.make_async_copy(w3_hbm, w3, sem3)
    for copy in copies2:
        copy.start()
    for i in range(3):
        w1[i, 3] = jnp.zeros((64, C1), BF16)
        for j in range(3):
            w1[i, j, 48:64, :] = jnp.zeros((16, C1), BF16)
    copy1.start()
    copy3.start()
    lat[2 * TM + t] = x_ref[...]

    pl.semaphore_wait(barrier, len(PEERS))
    for d, e in PEERS:
        pltpu.make_async_remote_copy(
            src_ref=x_ref,
            dst_ref=lat.at[(2 - d) * TM + t],
            send_sem=send_sem,
            recv_sem=recv_sem,
            device_id=away(d, e),
            device_id_type=MESH,
        ).start()

    for i in range(3):
        copies2[i].wait()

        @pl.loop(0, C1 // 32)
        def _(n):
            add_taps(w2, w2s, i, pl.ds(pl.multiple_of(32 * n, 32), 32))

    copy3.wait()

    @pl.loop(0, C2 // 32)
    def _(n):
        for i in range(3):
            add_taps(w3, w3s, i, pl.ds(pl.multiple_of(32 * n, 32), 32))

    copy1.wait()
    whole = lat.at[pl.ds(0, len(PEERS))]
    every = pltpu.make_async_remote_copy(
        src_ref=whole,
        dst_ref=whole,
        send_sem=send_sem,
        recv_sem=recv_sem,
        device_id=away(0, 1),
        device_id_type=MESH,
    )
    every.wait_recv()

    patches(lat, pat, s, t)
    lhs = []
    for r in range(3):
        q = jnp.clip(s - 1 + r, 0, SEQ - 1) - s + 1
        cols = []
        for i in range(3):
            for two in (0, 2):
                cols.append(pat[q + two, 32 * i : 32 * i + 192, :].astype(BF16))
        lhs.append(jnp.concatenate(cols, axis=1))
    lhs = jnp.concatenate(lhs, axis=0)
    hidden = jnp.dot(lhs, w1[...].reshape(768, C1), preferred_element_type=F32) + b1_ref[...]
    act = silu_normed(hidden, g1_ref[...])
    for r in range(3):
        x1[r] = act[192 * r : 192 * r + 192]

    lhs = jnp.concatenate(
        [
            x1[u : u + 2, 32 * i : 32 * i + 128, :].reshape(256, C1)
            for u in range(2)
            for i in range(3)
        ],
        axis=1,
    )
    col = lax.broadcasted_iota(jnp.int32, (256, 1), 0) % W
    for rp in range(2):
        q0, qk, q2 = [
            jnp.dot(lhs, tap_matrix(w2, w2s, rp, b), preferred_element_type=F32)
            for b in range(3)
        ]
        qk = qk + b2_ref[...]
        even = qk + jnp.where(col == 0, 0.0, pltpu.roll(q0, 1, 0) - q0)
        odd = qk + jnp.where(col == W - 1, 0.0, pltpu.roll(q2, 255, 0) - q2)
        for p, value in enumerate((even, odd)):
            act = silu_normed(value, g2_ref[...])
            for row in range(2):
                slot = 2 * row + 1 - rp
                for f in range(4):
                    part = act[128 * row + 32 * f : 128 * row + 32 * f + 32]
                    x2[slot, 64 * f + 32 * p : 64 * f + 32 * p + 32, :] = part

    slots = [jnp.where(s == 0, 1, 0), 1, 2, jnp.where(s == SEQ - 1, 2, 3)]
    col = lax.broadcasted_iota(jnp.int32, (32, 1), 0)
    for rp in range(2):
        lhs = jnp.concatenate(
            [
                jnp.concatenate(
                    [x2[slots[rp + u + row], 64 * i : 64 * i + 128, :] for row in range(2)],
                    axis=0,
                )
                for u in range(2)
                for i in range(3)
            ],
            axis=1,
        )
        rhs = jnp.concatenate([tap_matrix(w3, w3s, rp, b) for b in range(3)], axis=1)
        res = jnp.dot(lhs, rhs, preferred_element_type=F32)
        for row in range(2):
            for f in range(2):
                base = 128 * row + 64 * f
                (e0, ek, e2), (o0, ok, o2) = [
                    [
                        res[base + 32 * p : base + 32 * p + 32, C3 * b : C3 * b + C3]
                        for b in range(3)
                    ]
                    for p in range(2)
                ]
                ek = ek + b3_ref[...]
                ok = ok + b3_ref[...]
                values = (
                    ek + jnp.where(col == 0, 0.0, pltpu.roll(o0, 1, 0) - e0),
                    ek + (o2 - e2),
                    ok + (e0 - o0),
                    ok + jnp.where(col == W - 1, 0.0, pltpu.roll(e2, 31, 0) - o2),
                )
                for n, value in enumerate(values):
                    o32[f, 2 * row + rp, pl.ds(n, W, stride=4), :] = value
    out_ref[...] = o32[...].astype(BF16)

    every.wait_send()


def decode(x, w1, b1, g1, w2, b2, g2, w3, b3):
    vmem = pl.BlockSpec(memory_space=pltpu.VMEM)
    hbm = pl.BlockSpec(memory_space=pltpu.HBM)
    return pl.pallas_call(
        kernel,
        out_shape=jax.ShapeDtypeStruct((2, 4, 128, C3), BF16),
        in_specs=[vmem, hbm, vmem, vmem, hbm, vmem, vmem, hbm, vmem],
        out_specs=vmem,
        scratch_shapes=[
            pltpu.VMEM((5 * TM, 8, 128), BF16),
            pltpu.VMEM((3, 4, 64, C1), BF16),
            pltpu.VMEM((3, 3, 3, C1, C2), BF16),
            pltpu.VMEM((3, 8, C1, C2), BF16),
            pltpu.VMEM((3, 3, 3, C2, C3), BF16),
            pltpu.VMEM((3, 8, C2, C3), BF16),
            pltpu.VMEM((5, 8 * W, 128), F32),
            pltpu.VMEM((3, 6 * W, C1), BF16),
            pltpu.VMEM((4, 4 * 64, C2), BF16),
            pltpu.VMEM((2, 4, 128, C3), F32),
            pltpu.SemaphoreType.DMA,
            pltpu.SemaphoreType.DMA,
            pltpu.SemaphoreType.DMA,
            pltpu.SemaphoreType.DMA((3,)),
            pltpu.SemaphoreType.DMA,
        ],
        compiler_params=pltpu.CompilerParams(
            collective_id=0, has_side_effects=True, vmem_limit_bytes=56 << 20
        ),
        name="decode",
    )(x, w1, b1, g1, w2, b2, g2, w3, b3)


def per_device(latent, w1, b1, g1, w2, b2, g2, w3, b3):
    line = lambda v: v.reshape(1, -1)
    return decode(
        latent, w1.reshape(3, 3, 48, C1), line(b1), line(g1), w2, line(b2), line(g2), w3, line(b3)
    )


def solution(mesh):
    placed = (P(None, ("seq", "tm")), P(), P(), P(), P(), P(), P(), P(), P())
    return jax.shard_map(
        per_device,
        mesh=mesh,
        in_specs=placed,
        out_specs=P("tm", "seq", None, None),
        check_vma=False,
    )
```

time: 27.3 us -> 21.2 us (0.78)
  Pallas kernels: 27.2 us -> 19.4 us
  local copies, waits for them, and re-layouts: 0 us -> 1.67 us
    pallas_call x2 -> x1, Pallas kernels: 27.2 us -> 19.4 us  [decode(): pl.pallas_call(kernel, out_shape=jax.ShapeDtypeStruct((2, 4, 128, C3), BF...]
    unnamed x0 -> x1, local copies, waits for them, and re-layouts: none -> 1.67 us
where the time goes in v2:
time: 21.2 us; the launch traced here: 21 us
  Pallas kernels  19.4 us (92%)
  local copies, waits for them, and re-layouts  1.67 us (8%)
    pallas_call x1, Pallas kernels, decode(): pl.pallas_call(kernel, out_shape=jax.ShapeDtypeStruct((2, 4, 128, C3), BF...  19.4 us
    unnamed x1, local copies, waits for them, and re-layouts  1.67 us

profile of v2, /device:TPU:1, one launch (start us, length us, event | category | flops | bytes accessed | tf_op | source)
XLA Modules:
  0.0 21.0 jit_solution(13012924934244567598)
XLA Ops:
  0.0 19.4 %decode.1 = bf16[2,4,128,128]{3,2,1,0:T(8,128)(2,1)} custom-call(bf16[8,128]{1,0:T(8,128)(2,1)} %x_ref.1, bf16[3,3,48,512]{3,2,1,0:T(8,128)(2,1)} %bitcast.6, f32[1,512]{1,0:T(1,128)} %bitcast.7, f32[1,512]{1,0:T(1,128)} %bitcast.8, bf16[3,3,3,512,256]{4,3,2,1,0:T(8,128)(2,1)} %w2_hbm.1, f32[1,256]{1,0:T(1,128)} %bitcast.9, f32[1,256]{1,0:T(1,128)} %bitcast.10, ...), custom_call_target="tpu_custom_call" | custom-call | tf_op jit(solution)/shard_map/decode/pallas_call | solution.py:250
  19.4 1.7 %copy.11 = bf16[2,4,128,128]{3,2,1,0:T(8,128)(2,1)} copy(bf16[2,4,128,128]{3,2,1,0:T(8,128)(2,1)} %decode.1) | data formatting | bytes 524288

commit v3 on v2

--- a/solution.py
+++ b/solution.py
@@ -105,11 +105,19 @@
     s, t = lax.axis_index("seq"), lax.axis_index("tm")
 
     def away(d, e):
-        return (lax.rem(s + (d + SEQ), SEQ), lax.rem(t + e, TM))
+        return (s + d, lax.rem(t + e, TM))
+
+    def when_row(d):
+        if d == 0:
+            return lambda f: f()
+        return pl.when(s + d >= 0 if d < 0 else s + d < SEQ)
 
     barrier = pltpu.get_barrier_semaphore()
     for d, e in PEERS:
-        pl.semaphore_signal(barrier, inc=1, device_id=away(d, e), device_id_type=MESH)
+
+        @when_row(d)
+        def _():
+            pl.semaphore_signal(barrier, inc=1, device_id=away(d, e), device_id_type=MESH)
 
     copies2 = [pltpu.make_async_copy(w2_hbm.at[i], w2.at[i], sem2.at[i]) for i in range(3)]
     copy1 = pltpu.make_async_copy(
@@ -126,16 +134,31 @@
     copy3.start()
     lat[2 * TM + t] = x_ref[...]
 
-    pl.semaphore_wait(barrier, len(PEERS))
+    rows = 1 + jnp.minimum(s, 2) + jnp.minimum(SEQ - 1 - s, 2)
+    pl.semaphore_wait(barrier, TM * rows - 1)
     for d, e in PEERS:
-        pltpu.make_async_remote_copy(
-            src_ref=x_ref,
-            dst_ref=lat.at[(2 - d) * TM + t],
-            send_sem=send_sem,
-            recv_sem=recv_sem,
-            device_id=away(d, e),
+
+        @when_row(d)
+        def _():
+            pltpu.make_async_remote_copy(
+                src_ref=x_ref,
+                dst_ref=lat.at[(2 - d) * TM + t],
+                send_sem=send_sem.at[2 + d],
+                recv_sem=recv_sem.at[2 - d],
+                device_id=away(d, e),
+                device_id_type=MESH,
+            ).start()
+
+    def all_of(d):
+        some = lat.at[pl.ds(0, TM if d else TM - 1)]
+        return pltpu.make_async_remote_copy(
+            src_ref=some,
+            dst_ref=some,
+            send_sem=send_sem.at[2 + d],
+            recv_sem=recv_sem.at[2 + d],
+            device_id=away(0, 1),
             device_id_type=MESH,
-        ).start()
+        )
 
     for i in range(3):
         copies2[i].wait()
@@ -152,16 +175,11 @@
             add_taps(w3, w3s, i, pl.ds(pl.multiple_of(32 * n, 32), 32))
 
     copy1.wait()
-    whole = lat.at[pl.ds(0, len(PEERS))]
-    every = pltpu.make_async_remote_copy(
-        src_ref=whole,
-        dst_ref=whole,
-        send_sem=send_sem,
-        recv_sem=recv_sem,
-        device_id=away(0, 1),
-        device_id_type=MESH,
-    )
-    every.wait_recv()
+    for d in (0, 1, -1, 2, -2):
+
+        @when_row(d)
+        def _():
+            all_of(d).wait_recv()
 
     patches(lat, pat, s, t)
     lhs = []
@@ -241,7 +259,11 @@
                     o32[f, 2 * row + rp, pl.ds(n, W, stride=4), :] = value
     out_ref[...] = o32[...].astype(BF16)
 
-    every.wait_send()
+    for d in (0, 1, -1, 2, -2):
+
+        @when_row(d)
+        def _():
+            all_of(d).wait_send()
 
 
 def decode(x, w1, b1, g1, w2, b2, g2, w3, b3):
@@ -263,8 +285,8 @@
             pltpu.VMEM((3, 6 * W, C1), BF16),
             pltpu.VMEM((4, 4 * 64, C2), BF16),
             pltpu.VMEM((2, 4, 128, C3), F32),
-            pltpu.SemaphoreType.DMA,
-            pltpu.SemaphoreType.DMA,
+            pltpu.SemaphoreType.DMA((5,)),
+            pltpu.SemaphoreType.DMA((5,)),
             pltpu.SemaphoreType.DMA,
             pltpu.SemaphoreType.DMA((3,)),
             pltpu.SemaphoreType.DMA,

time: 21.2 us -> 18.5 us (0.87)
  the two profiles are of different devices: /device:TPU:1 before, /device:TPU:7 now
where the time goes in v3:
time: 18.5 us; the launch traced here: 18.4 us
  Pallas kernels  16.7 us (90%)
  local copies, waits for them, and re-layouts  1.67 us (9%)
    pallas_call x1, Pallas kernels, decode(): pl.pallas_call(kernel, out_shape=jax.ShapeDtypeStruct((2, 4, 128, C3), BF...  16.7 us
    unnamed x1, local copies, waits for them, and re-layouts  1.67 us

profile of v3, /device:TPU:7, one launch (start us, length us, event | category | flops | bytes accessed | tf_op | source)
XLA Modules:
  0.0 18.4 jit_solution(10896012791208132846)
XLA Ops:
  0.0 16.7 %decode.1 = bf16[2,4,128,128]{3,2,1,0:T(8,128)(2,1)} custom-call(bf16[8,128]{1,0:T(8,128)(2,1)} %x_ref.1, bf16[3,3,48,512]{3,2,1,0:T(8,128)(2,1)} %bitcast.6, f32[1,512]{1,0:T(1,128)} %bitcast.7, f32[1,512]{1,0:T(1,128)} %bitcast.8, bf16[3,3,3,512,256]{4,3,2,1,0:T(8,128)(2,1)} %w2_hbm.1, f32[1,256]{1,0:T(1,128)} %bitcast.9, f32[1,256]{1,0:T(1,128)} %bitcast.10, ...), custom_call_target="tpu_custom_call" | custom-call | tf_op jit(solution)/shard_map/decode/pallas_call | solution.py:272
  16.7 1.7 %copy.11 = bf16[2,4,128,128]{3,2,1,0:T(8,128)(2,1)} copy(bf16[2,4,128,128]{3,2,1,0:T(8,128)(2,1)} %decode.1) | data formatting | bytes 524288

commit v4 on v3

--- a/solution.py
+++ b/solution.py
@@ -97,10 +97,10 @@
     return jnp.concatenate(parts, axis=0)
 
 
-def kernel(
-    x_ref, w1_hbm, b1_ref, g1_ref, w2_hbm, b2_ref, g2_ref, w3_hbm, b3_ref,
-    out_ref,
-    lat, w1, w2, w2s, w3, w3s, pat, x1, x2, o32, send_sem, recv_sem, sem1, sem2, sem3,
+def gather_kernel(
+    x_ref, w1_hbm, w2_hbm, w3_hbm,
+    lat, w1, w2, w2s, w3, w3s,
+    send_sem, recv_sem, sem1, sem2, sem3,
 ):
     s, t = lax.axis_index("seq"), lax.axis_index("tm")
 
@@ -180,6 +180,20 @@
         @when_row(d)
         def _():
             all_of(d).wait_recv()
+
+    for d in (0, 1, -1, 2, -2):
+
+        @when_row(d)
+        def _():
+            all_of(d).wait_send()
+
+
+def decode_kernel(
+    lat, w1, w2, w2s, w3, w3s, b1_ref, g1_ref, b2_ref, g2_ref, b3_ref,
+    out_ref,
+    pat, x1, x2, o32,
+):
+    s, t = lax.axis_index("seq"), lax.axis_index("tm")
 
     patches(lat, pat, s, t)
     lhs = []
@@ -259,32 +273,25 @@
                     o32[f, 2 * row + rp, pl.ds(n, W, stride=4), :] = value
     out_ref[...] = o32[...].astype(BF16)
 
-    for d in (0, 1, -1, 2, -2):
-
-        @when_row(d)
-        def _():
-            all_of(d).wait_send()
-
-
-def decode(x, w1, b1, g1, w2, b2, g2, w3, b3):
+
+def per_device(latent, w1, b1, g1, w2, b2, g2, w3, b3):
+    line = lambda v: v.reshape(1, -1)
     vmem = pl.BlockSpec(memory_space=pltpu.VMEM)
     hbm = pl.BlockSpec(memory_space=pltpu.HBM)
-    return pl.pallas_call(
-        kernel,
-        out_shape=jax.ShapeDtypeStruct((2, 4, 128, C3), BF16),
-        in_specs=[vmem, hbm, vmem, vmem, hbm, vmem, vmem, hbm, vmem],
-        out_specs=vmem,
-        scratch_shapes=[
+    in_hbm = lambda v: pltpu.with_memory_space_constraint(v, pltpu.HBM)
+    kept = pl.pallas_call(
+        gather_kernel,
+        out_shape=[
             pltpu.VMEM((5 * TM, 8, 128), BF16),
             pltpu.VMEM((3, 4, 64, C1), BF16),
             pltpu.VMEM((3, 3, 3, C1, C2), BF16),
             pltpu.VMEM((3, 8, C1, C2), BF16),
             pltpu.VMEM((3, 3, 3, C2, C3), BF16),
             pltpu.VMEM((3, 8, C2, C3), BF16),
-            pltpu.VMEM((5, 8 * W, 128), F32),
-            pltpu.VMEM((3, 6 * W, C1), BF16),
-            pltpu.VMEM((4, 4 * 64, C2), BF16),
-            pltpu.VMEM((2, 4, 128, C3), F32),
+        ],
+        in_specs=[vmem, hbm, hbm, hbm],
+        out_specs=[vmem] * 6,
+        scratch_shapes=[
             pltpu.SemaphoreType.DMA((5,)),
             pltpu.SemaphoreType.DMA((5,)),
             pltpu.SemaphoreType.DMA,
@@ -292,17 +299,24 @@
             pltpu.SemaphoreType.DMA,
         ],
         compiler_params=pltpu.CompilerParams(
-            collective_id=0, has_side_effects=True, vmem_limit_bytes=56 << 20
+            collective_id=0, has_side_effects=True, vmem_limit_bytes=8 << 20
         ),
+        name="gather",
+    )(*map(in_hbm, (latent, w1.reshape(3, 3, 48, C1), w2, w3)))
+    return pl.pallas_call(
+        decode_kernel,
+        out_shape=jax.ShapeDtypeStruct((2, 4, 128, C3), BF16),
+        in_specs=[vmem] * 11,
+        out_specs=vmem,
+        scratch_shapes=[
+            pltpu.VMEM((5, 8 * W, 128), F32),
+            pltpu.VMEM((3, 6 * W, C1), BF16),
+            pltpu.VMEM((4, 4 * 64, C2), BF16),
+            pltpu.VMEM((2, 4, 128, C3), F32),
+        ],
+        compiler_params=pltpu.CompilerParams(vmem_limit_bytes=24 << 20),
         name="decode",
-    )(x, w1, b1, g1, w2, b2, g2, w3, b3)
-
-
-def per_device(latent, w1, b1, g1, w2, b2, g2, w3, b3):
-    line = lambda v: v.reshape(1, -1)
-    return decode(
-        latent, w1.reshape(3, 3, 48, C1), line(b1), line(g1), w2, line(b2), line(g2), w3, line(b3)
-    )
+    )(*kept, line(b1), line(g1), line(b2), line(g2), line(b3))
 
 
 def solution(mesh):

time: 18.5 us -> 17.1 us (0.924)
  local copies, waits for them, and re-layouts: 1.67 us -> 0.02 us
  Pallas kernels: 16.7 us -> 16.9 us
    unnamed x1 -> x10, local copies, waits for them, and re-layouts: 1.67 us -> 0.02 us
    pallas_call x1 -> x2, Pallas kernels: 16.7 us -> 16.9 us  [the longest x1 11 us: per_device(): pl.pallas_call(gather_kernel, out_shape=[pltpu.VMEM((5 * TM, 8, 128), BF1...]
where the time goes in v4:
time: 17.1 us; the launch traced here: 17 us
  Pallas kernels  16.9 us (99%)
    pallas_call x1, Pallas kernels, per_device(): pl.pallas_call(gather_kernel, out_shape=[pltpu.VMEM((5 * TM, 8, 128), BF1...  11 us
    pallas_call x1, Pallas kernels, per_device(): pl.pallas_call(decode_kernel, out_shape=jax.ShapeDtypeStruct((2, 4, 128,...  5.9 us

profile of v4, /device:TPU:7, one launch (start us, length us, event | category | flops | bytes accessed | tf_op | source)
XLA Modules:
  0.0 17.0 jit_solution(9487192608515749843)
XLA Ops:
  0.0 0.0 copy-start.4
  0.0 0.0 copy-start.3
  0.0 0.0 copy-start.2
  0.0 0.0 copy-start.1
  0.0 0.0 copy-start
  0.0 11.0 %gather.1 = (bf16[20,8,128]{2,1,0:T(8,128)(2,1)S(1)}, bf16[3,4,64,512]{3,2,1,0:T(8,128)(2,1)S(1)}, bf16[3,3,3,512,256]{4,3,2,1,0:T(8,128)(2,1)S(1)}, bf16[3,8,51...) custom-call(bf16[8,128]{1,0:T(8,128)(2,1)} %x_ref.1, ...), custom_call_target="tpu_custom_call" | custom-call | tf_op jit(solution)/shard_map/gather/pallas_call | solution.py:282
  11.0 0.0 copy-done.4
  11.0 0.0 copy-done.3
  11.0 0.0 copy-done.2
  11.0 0.0 copy-done.1
  11.1 0.0 copy-done
  11.1 5.9 %decode.1 = bf16[2,4,128,128]{3,2,1,0:T(8,128)(2,1)} custom-call(bf16[20,8,128]{2,1,0:T(8,128)(2,1)S(1)} %get-tuple-element.11.lat, bf16[3,4,64,512]{3,2,1,0:T(8,128)(2,1)S(1)} %get-tuple-element.12.w1, bf16[3,3,3,512,256]{4,3,2,1,0:T(8,128)(2,1)S(1)} %get-tuple-element.13.w2, bf16[3,8,512,256]{3,2,1,0:T(8,128)(2,1)S(1)} %get-tuple-element.14.w2s, ...), custom_call_target="tpu_custom_call" | custom-call | tf_op jit(solution)/shard_map/decode/pallas_call | solution.py:306
Async XLA Ops:
  0.0 11.0 %copy-start.4 = (f32[128]{0:T(128)S(1)}, f32[128]{0:T(128)}, u32[]{:S(2)}) copy-start(f32[128]{0:T(128)} %param.17) | copy-start | bytes 1540
  0.0 11.0 %copy-start.3 = (f32[256]{0:T(256)S(1)}, f32[256]{0:T(256)}, u32[]{:S(2)}) copy-start(f32[256]{0:T(256)} %param.15) | copy-start | bytes 3076
  0.0 11.0 %copy-start.2 = (f32[256]{0:T(256)S(1)}, f32[256]{0:T(256)}, u32[]{:S(2)}) copy-start(f32[256]{0:T(256)} %param.14) | copy-start | bytes 3076
  0.0 11.0 %copy-start.1 = (f32[512]{0:T(512)S(1)}, f32[512]{0:T(512)}, u32[]{:S(2)}) copy-start(f32[512]{0:T(512)} %param.12) | copy-start | bytes 6148
  0.0 11.0 %copy-start = (f32[512]{0:T(512)S(1)}, f32[512]{0:T(512)}, u32[]{:S(2)}) copy-start(f32[512]{0:T(512)} %param.11) | copy-start | bytes 6148

commit v5 on v4

--- a/solution.py
+++ b/solution.py
@@ -70,18 +70,21 @@
             pat_ref[q, pl.ds(c, 8, stride=W), :] = jnp.where(lane < 48, low, high)
 
 
-def sums(taps):
-    r12 = [taps[1, k] + taps[2, k] for k in range(3)]
-    r01 = [taps[0, k] + taps[1, k] for k in range(3)]
-    k0 = [taps[0, k] for k in range(3)]
-    k2 = [taps[2, k] for k in range(3)]
-    total = lambda r: r[0] + r[1] + r[2]
-    return (total(k0), r12[0], total(r12), r12[2], r01[0], total(r01), r01[2], total(k2))
-
-
 def add_taps(raw, summed, i, rows):
-    taps = {(j, k): raw[i, j, k, rows, :].astype(F32) for j in range(3) for k in range(3)}
-    for n, value in enumerate(sums(taps)):
+    taps = {(j, k): raw[i, j, k, rows, :] for j in range(3) for k in range(3)}
+    wide = {place: value.astype(F32) for place, value in taps.items()}
+    total = [wide[j, 0] + wide[j, 1] + wide[j, 2] for j in range(3)]
+    values = (
+        total[0],
+        taps[1, 0] + taps[2, 0],
+        total[1] + total[2],
+        taps[1, 2] + taps[2, 2],
+        taps[0, 0] + taps[1, 0],
+        total[0] + total[1],
+        taps[0, 2] + taps[1, 2],
+        total[2],
+    )
+    for n, value in enumerate(values):
         summed[i, n, rows, :] = value.astype(BF16)
 
 
@@ -98,9 +101,9 @@
 
 
 def gather_kernel(
-    x_ref, w1_hbm, w2_hbm, w3_hbm,
+    x_hbm, w1_hbm, w2_hbm, w3_hbm,
     lat, w1, w2, w2s, w3, w3s,
-    send_sem, recv_sem, sem1, sem2, sem3,
+    send_sem, recv_sem, own_sem, sem1, sem2, sem3,
 ):
     s, t = lax.axis_index("seq"), lax.axis_index("tm")
 
@@ -119,29 +122,33 @@
         def _():
             pl.semaphore_signal(barrier, inc=1, device_id=away(d, e), device_id_type=MESH)
 
+    own = lat.at[2 * TM + t]
+    own_copy = pltpu.make_async_copy(x_hbm, own, own_sem)
+    own_copy.start()
+
     copies2 = [pltpu.make_async_copy(w2_hbm.at[i], w2.at[i], sem2.at[i]) for i in range(3)]
     copy1 = pltpu.make_async_copy(
         w1_hbm, w1.at[:, pl.ds(0, 3), pl.ds(0, 48), :], sem1
     )
     copy3 = pltpu.make_async_copy(w3_hbm, w3, sem3)
     for copy in copies2:
-        copy.start()
+        copy.start(priority=1)
     for i in range(3):
         w1[i, 3] = jnp.zeros((64, C1), BF16)
         for j in range(3):
             w1[i, j, 48:64, :] = jnp.zeros((16, C1), BF16)
-    copy1.start()
-    copy3.start()
-    lat[2 * TM + t] = x_ref[...]
+    copy1.start(priority=1)
+    copy3.start(priority=1)
 
     rows = 1 + jnp.minimum(s, 2) + jnp.minimum(SEQ - 1 - s, 2)
+    own_copy.wait()
     pl.semaphore_wait(barrier, TM * rows - 1)
     for d, e in PEERS:
 
         @when_row(d)
         def _():
             pltpu.make_async_remote_copy(
-                src_ref=x_ref,
+                src_ref=own,
                 dst_ref=lat.at[(2 - d) * TM + t],
                 send_sem=send_sem.at[2 + d],
                 recv_sem=recv_sem.at[2 - d],
@@ -163,9 +170,9 @@
     for i in range(3):
         copies2[i].wait()
 
-        @pl.loop(0, C1 // 32)
+        @pl.loop(0, C1 // 64)
         def _(n):
-            add_taps(w2, w2s, i, pl.ds(pl.multiple_of(32 * n, 32), 32))
+            add_taps(w2, w2s, i, pl.ds(pl.multiple_of(64 * n, 64), 64))
 
     copy3.wait()
 
@@ -188,37 +195,37 @@
             all_of(d).wait_send()
 
 
-def decode_kernel(
-    lat, w1, w2, w2s, w3, w3s, b1_ref, g1_ref, b2_ref, g2_ref, b3_ref,
-    out_ref,
-    pat, x1, x2, o32,
-):
-    s, t = lax.axis_index("seq"), lax.axis_index("tm")
-
-    patches(lat, pat, s, t)
+def convolutions(s, pat, w1, w2, w2s, b1_ref, g1_ref, b2_ref, g2_ref, x1, x2, first):
+    start = 4 if first else 0
+    size = W * (6 - start)
     lhs = []
     for r in range(3):
         q = jnp.clip(s - 1 + r, 0, SEQ - 1) - s + 1
         cols = []
         for i in range(3):
             for two in (0, 2):
-                cols.append(pat[q + two, 32 * i : 32 * i + 192, :].astype(BF16))
+                at = W * (i + start)
+                cols.append(pat[q + two, at : at + size, :].astype(BF16))
         lhs.append(jnp.concatenate(cols, axis=1))
     lhs = jnp.concatenate(lhs, axis=0)
     hidden = jnp.dot(lhs, w1[...].reshape(768, C1), preferred_element_type=F32) + b1_ref[...]
     act = silu_normed(hidden, g1_ref[...])
     for r in range(3):
-        x1[r] = act[192 * r : 192 * r + 192]
-
+        x1[r, W * start : W * 6, :] = act[size * r : size * r + size]
+        for k in range(first, start):
+            x1[r, W * k : W * k + W, :] = act[size * r : size * r + W]
+
+    frames = 4 - first
+    size = W * frames
     lhs = jnp.concatenate(
         [
-            x1[u : u + 2, 32 * i : 32 * i + 128, :].reshape(256, C1)
+            x1[u : u + 2, W * (i + first) : W * (i + first) + size, :].reshape(2 * size, C1)
             for u in range(2)
             for i in range(3)
         ],
         axis=1,
     )
-    col = lax.broadcasted_iota(jnp.int32, (256, 1), 0) % W
+    col = lax.broadcasted_iota(jnp.int32, (2 * size, 1), 0) % W
     for rp in range(2):
         q0, qk, q2 = [
             jnp.dot(lhs, tap_matrix(w2, w2s, rp, b), preferred_element_type=F32)
@@ -226,14 +233,37 @@
         ]
         qk = qk + b2_ref[...]
         even = qk + jnp.where(col == 0, 0.0, pltpu.roll(q0, 1, 0) - q0)
-        odd = qk + jnp.where(col == W - 1, 0.0, pltpu.roll(q2, 255, 0) - q2)
+        odd = qk + jnp.where(col == W - 1, 0.0, pltpu.roll(q2, 2 * size - 1, 0) - q2)
         for p, value in enumerate((even, odd)):
             act = silu_normed(value, g2_ref[...])
             for row in range(2):
                 slot = 2 * row + 1 - rp
-                for f in range(4):
-                    part = act[128 * row + 32 * f : 128 * row + 32 * f + 32]
-                    x2[slot, 64 * f + 32 * p : 64 * f + 32 * p + 32, :] = part
+                for f in range(frames):
+                    part = act[size * row + W * f : size * row + W * f + W]
+                    at = 64 * (f + first) + W * p
+                    x2[slot, at : at + W, :] = part
+
+
+def decode_kernel(
+    lat, w1, w2, w2s, w3, w3s, b1_ref, g1_ref, b2_ref, g2_ref, b3_ref,
+    out_ref,
+    pat, x1, x2, o32,
+):
+    s, t = lax.axis_index("seq"), lax.axis_index("tm")
+
+    patches(lat, pat, s, t)
+
+    @pl.when(t == 0)
+    def _():
+        convolutions(s, pat, w1, w2, w2s, b1_ref, g1_ref, b2_ref, g2_ref, x1, x2, 2)
+        for slot in range(4):
+            third = x2[slot, 128:192, :]
+            x2[slot, 0:64, :] = third
+            x2[slot, 64:128, :] = third
+
+    @pl.when(t > 0)
+    def _():
+        convolutions(s, pat, w1, w2, w2s, b1_ref, g1_ref, b2_ref, g2_ref, x1, x2, 0)
 
     slots = [jnp.where(s == 0, 1, 0), 1, 2, jnp.where(s == SEQ - 1, 2, 3)]
     col = lax.broadcasted_iota(jnp.int32, (32, 1), 0)
@@ -289,11 +319,12 @@
             pltpu.VMEM((3, 3, 3, C2, C3), BF16),
             pltpu.VMEM((3, 8, C2, C3), BF16),
         ],
-        in_specs=[vmem, hbm, hbm, hbm],
+        in_specs=[hbm] * 4,
         out_specs=[vmem] * 6,
         scratch_shapes=[
             pltpu.SemaphoreType.DMA((5,)),
             pltpu.SemaphoreType.DMA((5,)),
+            pltpu.SemaphoreType.DMA,
             pltpu.SemaphoreType.DMA,
             pltpu.SemaphoreType.DMA((3,)),
             pltpu.SemaphoreType.DMA,

time: 17.1 us -> 15.7 us (0.918)
  the two profiles are of different devices: /device:TPU:7 before, /device:TPU:15 now
where the time goes in v5:
time: 15.7 us; the launch traced here: 15.6 us
  Pallas kernels  15.5 us (99%)
    pallas_call x1, Pallas kernels, per_device(): pl.pallas_call(gather_kernel, out_shape=[pltpu.VMEM((5 * TM, 8, 128), BF1...  9.56 us
    pallas_call x1, Pallas kernels, per_device(): pl.pallas_call(decode_kernel, out_shape=jax.ShapeDtypeStruct((2, 4, 128,...  5.96 us

profile of v5, /device:TPU:15, one launch (start us, length us, event | category | flops | bytes accessed | tf_op | source)
XLA Modules:
  0.0 15.6 jit_solution(5526378945105021743)
XLA Ops:
  0.0 0.0 copy-start.4
  0.0 0.0 copy-start.3
  0.0 0.0 copy-start.2
  0.0 0.0 copy-start.1
  0.0 0.0 copy-start
  0.0 9.6 %gather.1 = (bf16[20,8,128]{2,1,0:T(8,128)(2,1)S(1)}, bf16[3,4,64,512]{3,2,1,0:T(8,128)(2,1)S(1)}, bf16[3,3,3,512,256]{4,3,2,1,0:T(8,128)(2,1)S(1)}, bf16[3,8,51...) custom-call(bf16[8,128]{1,0:T(8,128)(2,1)} %x_hbm.1, ...), custom_call_target="tpu_custom_call" | custom-call | tf_op jit(solution)/shard_map/gather/pallas_call | solution.py:312
  9.6 0.0 copy-done.4
  9.6 0.0 copy-done.3
  9.6 0.0 copy-done.2
  9.6 0.0 copy-done.1
  9.6 0.0 copy-done
  9.6 6.0 %decode.1 = bf16[2,4,128,128]{3,2,1,0:T(8,128)(2,1)} custom-call(bf16[20,8,128]{2,1,0:T(8,128)(2,1)S(1)} %get-tuple-element.11.lat, bf16[3,4,64,512]{3,2,1,0:T(8,128)(2,1)S(1)} %get-tuple-element.12.w1, bf16[3,3,3,512,256]{4,3,2,1,0:T(8,128)(2,1)S(1)} %get-tuple-element.13.w2, bf16[3,8,512,256]{3,2,1,0:T(8,128)(2,1)S(1)} %get-tuple-element.14.w2s, ...), custom_call_target="tpu_custom_call" | custom-call | tf_op jit(solution)/shard_map/decode/pallas_call | solution.py:337
Async XLA Ops:
  0.0 9.6 %copy-start.4 = (f32[128]{0:T(128)S(1)}, f32[128]{0:T(128)}, u32[]{:S(2)}) copy-start(f32[128]{0:T(128)} %param.17) | copy-start | bytes 1540
  0.0 9.6 %copy-start.3 = (f32[256]{0:T(256)S(1)}, f32[256]{0:T(256)}, u32[]{:S(2)}) copy-start(f32[256]{0:T(256)} %param.15) | copy-start | bytes 3076
  0.0 9.6 %copy-start.2 = (f32[256]{0:T(256)S(1)}, f32[256]{0:T(256)}, u32[]{:S(2)}) copy-start(f32[256]{0:T(256)} %param.14) | copy-start | bytes 3076
  0.0 9.6 %copy-start.1 = (f32[512]{0:T(512)S(1)}, f32[512]{0:T(512)}, u32[]{:S(2)}) copy-start(f32[512]{0:T(512)} %param.12) | copy-start | bytes 6148
  0.0 9.6 %copy-start = (f32[512]{0:T(512)S(1)}, f32[512]{0:T(512)}, u32[]{:S(2)}) copy-start(f32[512]{0:T(512)} %param.11) | copy-start | bytes 6148

commit v6 on v5

--- a/solution.py
+++ b/solution.py
@@ -12,11 +12,14 @@
 SEQ = 32
 TM = 4
 W = 32
+CHUNK = 16
 C1, C2, C3 = 512, 256, 128
 EPS = 1e-06
 
 RAW = {(0, 0, 0): (0, 0), (0, 0, 2): (0, 2), (1, 1, 0): (2, 0), (1, 1, 2): (2, 2)}
 SUMS = ((0, 0, 1), (0, 1, 0), (0, 1, 1), (0, 1, 2), (1, 0, 0), (1, 0, 1), (1, 0, 2), (1, 1, 1))
+PLACES = SUMS + tuple(RAW)
+KEPT = tuple((n, p) for n in range(4) for p in (SUMS if n in (0, 3) else PLACES))
 PEERS = tuple(
     (d, e) for d, e in (
         (2, 2), (-2, 2), (1, 2), (-1, 2), (2, 1), (2, 3), (-2, 1), (-2, 3), (0, 2), (1, 1), (1, 3),
@@ -70,22 +73,28 @@
             pat_ref[q, pl.ds(c, 8, stride=W), :] = jnp.where(lane < 48, low, high)
 
 
+def merged(taps):
+    wide = {place: value.astype(F32) for place, value in taps.items()}
+    total = [wide[j, 0] + wide[j, 1] + wide[j, 2] for j in range(3)]
+    values = {
+        (0, 0, 1): total[0],
+        (0, 1, 0): wide[1, 0] + wide[2, 0],
+        (0, 1, 1): total[1] + total[2],
+        (0, 1, 2): wide[1, 2] + wide[2, 2],
+        (1, 0, 0): wide[0, 0] + wide[1, 0],
+        (1, 0, 1): total[0] + total[1],
+        (1, 0, 2): wide[0, 2] + wide[1, 2],
+        (1, 1, 1): total[2],
+    }
+    values.update({p: wide[tap] for p, tap in RAW.items()})
+    return values
+
+
 def add_taps(raw, summed, i, rows):
     taps = {(j, k): raw[i, j, k, rows, :] for j in range(3) for k in range(3)}
-    wide = {place: value.astype(F32) for place, value in taps.items()}
-    total = [wide[j, 0] + wide[j, 1] + wide[j, 2] for j in range(3)]
-    values = (
-        total[0],
-        taps[1, 0] + taps[2, 0],
-        total[1] + total[2],
-        taps[1, 2] + taps[2, 2],
-        taps[0, 0] + taps[1, 0],
-        total[0] + total[1],
-        taps[0, 2] + taps[1, 2],
-        total[2],
-    )
-    for n, value in enumerate(values):
-        summed[i, n, rows, :] = value.astype(BF16)
+    values = merged(taps)
+    for n, p in enumerate(SUMS):
+        summed[i, n, rows, :] = values[p].astype(BF16)
 
 
 def tap_matrix(raw, summed, rp, b):
@@ -100,6 +109,31 @@
     return jnp.concatenate(parts, axis=0)
 
 
+def add_timed_taps(raw, summed, rows, lanes):
+    steps = [
+        merged({(j, k): raw[i, j, k, rows, lanes] for j in range(3) for k in range(3)})
+        for i in range(3)
+    ]
+    for p in PLACES:
+        g0, g1, g2 = (step[p] for step in steps)
+        outer, inner = 0.5 * (g0 + g2), 0.5 * g1
+        for n, value in enumerate((g0, outer + inner, outer - inner, g2)):
+            if (n, p) in KEPT:
+                summed[KEPT.index((n, p)), rows, lanes] = value.astype(BF16)
+
+
+def timed_matrix(raw, summed, rp, b, n):
+    parts = []
+    for u in range(2):
+        p = (rp, u, b)
+        if (n, p) in KEPT:
+            parts.append(summed[KEPT.index((n, p))])
+        else:
+            j, k = RAW[p]
+            parts.append(raw[0 if n == 0 else 2, j, k])
+    return jnp.concatenate(parts, axis=0)
+
+
 def gather_kernel(
     x_hbm, w1_hbm, w2_hbm, w3_hbm,
     lat, w1, w2, w2s, w3, w3s,
@@ -126,7 +160,13 @@
     own_copy = pltpu.make_async_copy(x_hbm, own, own_sem)
     own_copy.start()
 
-    copies2 = [pltpu.make_async_copy(w2_hbm.at[i], w2.at[i], sem2.at[i]) for i in range(3)]
+    parts = [pl.ds(128 * i, 128) for i in range(C1 // 128)]
+    copies2 = [
+        pltpu.make_async_copy(
+            w2_hbm.at[:, :, :, part, :], w2.at[:, :, :, part, :], sem2.at[i]
+        )
+        for i, part in enumerate(parts)
+    ]
     copy1 = pltpu.make_async_copy(
         w1_hbm, w1.at[:, pl.ds(0, 3), pl.ds(0, 48), :], sem1
     )
@@ -167,12 +207,14 @@
             device_id_type=MESH,
         )
 
-    for i in range(3):
-        copies2[i].wait()
-
-        @pl.loop(0, C1 // 64)
+    for i, copy in enumerate(copies2):
+        copy.wait()
+
+        @pl.loop(0, 128 // CHUNK)
         def _(n):
-            add_taps(w2, w2s, i, pl.ds(pl.multiple_of(64 * n, 64), 64))
+            rows = pl.ds(pl.multiple_of(128 * i + CHUNK * n, CHUNK), CHUNK)
+            for lane in range(0, C2, 128):
+                add_timed_taps(w2, w2s, rows, pl.ds(lane, 128))
 
     copy3.wait()
 
@@ -198,7 +240,6 @@
 def convolutions(s, pat, w1, w2, w2s, b1_ref, g1_ref, b2_ref, g2_ref, x1, x2, first):
     start = 4 if first else 0
     size = W * (6 - start)
-    lhs = []
     for r in range(3):
         q = jnp.clip(s - 1 + r, 0, SEQ - 1) - s + 1
         cols = []
@@ -206,42 +247,53 @@
             for two in (0, 2):
                 at = W * (i + start)
                 cols.append(pat[q + two, at : at + size, :].astype(BF16))
-        lhs.append(jnp.concatenate(cols, axis=1))
-    lhs = jnp.concatenate(lhs, axis=0)
-    hidden = jnp.dot(lhs, w1[...].reshape(768, C1), preferred_element_type=F32) + b1_ref[...]
-    act = silu_normed(hidden, g1_ref[...])
-    for r in range(3):
-        x1[r, W * start : W * 6, :] = act[size * r : size * r + size]
+        lhs = jnp.concatenate(cols, axis=1)
+        hidden = jnp.dot(lhs, w1[...].reshape(768, C1), preferred_element_type=F32)
+        act = silu_normed(hidden + b1_ref[...], g1_ref[...])
+        kinds = (1, 3) if first else (0, 1, 2, 3)
+        d = {k: act[W * (k - start) : W * (k - start) + W] for k in range(start, 6)}
         for k in range(first, start):
-            x1[r, W * k : W * k + W, :] = act[size * r : size * r + W]
-
-    frames = 4 - first
-    size = W * frames
-    lhs = jnp.concatenate(
-        [
-            x1[u : u + 2, W * (i + first) : W * (i + first) + size, :].reshape(2 * size, C1)
-            for u in range(2)
-            for i in range(3)
-        ],
-        axis=1,
-    )
+            d[k] = d[start]
+        for f in range(first, 4, 2):
+            terms = (d[f] - d[f + 2], d[f + 1] + d[f + 2], d[f + 2] - d[f + 1], d[f + 1] - d[f + 3])
+            for n in kinds:
+                x1[n, r, W // 2 * f : W // 2 * f + W, :] = terms[n]
+
+    size = W * (4 - first) // 2
+    lhs = {
+        n: jnp.concatenate(
+            [
+                x1[n, u : u + 2, W // 2 * first : 2 * W, :].reshape(2 * size, C1)
+                for u in range(2)
+            ],
+            axis=1,
+        )
+        for n in kinds
+    }
     col = lax.broadcasted_iota(jnp.int32, (2 * size, 1), 0) % W
+
+    def two_frames(rp, b):
+        m = {
+            n: jnp.dot(lhs[n], timed_matrix(w2, w2s, rp, b, n), preferred_element_type=F32)
+            for n in kinds
+        }
+        if first:
+            return m[1], m[1] - m[3]
+        return m[0] + (m[1] + m[2]), (m[1] - m[2]) - m[3]
+
     for rp in range(2):
-        q0, qk, q2 = [
-            jnp.dot(lhs, tap_matrix(w2, w2s, rp, b), preferred_element_type=F32)
-            for b in range(3)
-        ]
-        qk = qk + b2_ref[...]
-        even = qk + jnp.where(col == 0, 0.0, pltpu.roll(q0, 1, 0) - q0)
-        odd = qk + jnp.where(col == W - 1, 0.0, pltpu.roll(q2, 2 * size - 1, 0) - q2)
-        for p, value in enumerate((even, odd)):
-            act = silu_normed(value, g2_ref[...])
-            for row in range(2):
-                slot = 2 * row + 1 - rp
-                for f in range(frames):
-                    part = act[size * row + W * f : size * row + W * f + W]
-                    at = 64 * (f + first) + W * p
-                    x2[slot, at : at + W, :] = part
+        for later, (q0, qk, q2) in enumerate(zip(*[two_frames(rp, b) for b in range(3)])):
+            qk = qk + b2_ref[...]
+            even = qk + jnp.where(col == 0, 0.0, pltpu.roll(q0, 1, 0) - q0)
+            odd = qk + jnp.where(col == W - 1, 0.0, pltpu.roll(q2, 2 * size - 1, 0) - q2)
+            for p, value in enumerate((even, odd)):
+                act = silu_normed(value, g2_ref[...])
+                for row in range(2):
+                    slot = 2 * row + 1 - rp
+                    for f in range(first, 4, 2):
+                        part = act[size * row + W // 2 * (f - first) :][:W]
+                        at = 64 * (f + later) + W * p
+                        x2[slot, at : at + W, :] = part
 
 
 def decode_kernel(
@@ -315,7 +367,7 @@
             pltpu.VMEM((5 * TM, 8, 128), BF16),
             pltpu.VMEM((3, 4, 64, C1), BF16),
             pltpu.VMEM((3, 3, 3, C1, C2), BF16),
-            pltpu.VMEM((3, 8, C1, C2), BF16),
+            pltpu.VMEM((len(KEPT), C1, C2), BF16),
             pltpu.VMEM((3, 3, 3, C2, C3), BF16),
             pltpu.VMEM((3, 8, C2, C3), BF16),
         ],
@@ -326,7 +378,7 @@
             pltpu.SemaphoreType.DMA((5,)),
             pltpu.SemaphoreType.DMA,
             pltpu.SemaphoreType.DMA,
-            pltpu.SemaphoreType.DMA((3,)),
+            pltpu.SemaphoreType.DMA((C1 // 128,)),
             pltpu.SemaphoreType.DMA,
         ],
         compiler_params=pltpu.CompilerParams(
@@ -341,7 +393,7 @@
         out_specs=vmem,
         scratch_shapes=[
             pltpu.VMEM((5, 8 * W, 128), F32),
-            pltpu.VMEM((3, 6 * W, C1), BF16),
+            pltpu.VMEM((4, 3, 2 * W, C1), BF16),
             pltpu.VMEM((4, 4 * 64, C2), BF16),
             pltpu.VMEM((2, 4, 128, C3), F32),
         ],

time: 15.7 us -> 15.3 us (0.975)
  Pallas kernels: 15.5 us -> 15 us
    pallas_call x1, Pallas kernels: 5.96 us -> 5.42 us  [per_device(): pl.pallas_call(decode_kernel, out_shape=jax.ShapeDtypeStruct((2, 4, 128,...]
where the time goes in v6:
time: 15.3 us; the launch traced here: 15.1 us
  Pallas kernels  15 us (98%)
    pallas_call x1, Pallas kernels, per_device(): pl.pallas_call(gather_kernel, out_shape=[pltpu.VMEM((5 * TM, 8, 128), BF1...  9.57 us
    pallas_call x1, Pallas kernels, per_device(): pl.pallas_call(decode_kernel, out_shape=jax.ShapeDtypeStruct((2, 4, 128,...  5.42 us

profile of v6, /device:TPU:15, one launch (start us, length us, event | category | flops | bytes accessed | tf_op | source)
XLA Modules:
  0.0 15.1 jit_solution(17882611363854351282)
XLA Ops:
  0.0 0.0 copy-start.4
  0.0 0.0 copy-start.3
  0.0 0.0 copy-start.2
  0.0 0.0 copy-start.1
  0.0 0.0 copy-start
  0.0 9.6 %gather.1 = (bf16[20,8,128]{2,1,0:T(8,128)(2,1)S(1)}, bf16[3,4,64,512]{3,2,1,0:T(8,128)(2,1)S(1)}, bf16[3,3,3,512,256]{4,3,2,1,0:T(8,128)(2,1)S(1)}, bf16[40,512...) custom-call(bf16[8,128]{1,0:T(8,128)(2,1)} %x_hbm.1, ...), custom_call_target="tpu_custom_call" | custom-call | tf_op jit(solution)/shard_map/gather/pallas_call | solution.py:364
  9.6 0.0 copy-done.4
  9.6 0.0 copy-done.3
  9.6 0.0 copy-done.2
  9.6 0.0 copy-done.1
  9.6 0.0 copy-done
  9.7 5.4 %decode.1 = bf16[2,4,128,128]{3,2,1,0:T(8,128)(2,1)} custom-call(bf16[20,8,128]{2,1,0:T(8,128)(2,1)S(1)} %get-tuple-element.11.lat, bf16[3,4,64,512]{3,2,1,0:T(8,128)(2,1)S(1)} %get-tuple-element.12.w1, bf16[3,3,3,512,256]{4,3,2,1,0:T(8,128)(2,1)S(1)} %get-tuple-element.13.w2, bf16[40,512,256]{2,1,0:T(8,128)(2,1)S(1)} %get-tuple-element.14.w2s, ...), custom_call_target="tpu_custom_call" | custom-call | tf_op jit(solution)/shard_map/decode/pallas_call | solution.py:389
Async XLA Ops:
  0.0 9.6 %copy-start.4 = (f32[128]{0:T(128)S(1)}, f32[128]{0:T(128)}, u32[]{:S(2)}) copy-start(f32[128]{0:T(128)} %param.17) | copy-start | bytes 1540
  0.0 9.6 %copy-start.3 = (f32[256]{0:T(256)S(1)}, f32[256]{0:T(256)}, u32[]{:S(2)}) copy-start(f32[256]{0:T(256)} %param.15) | copy-start | bytes 3076
  0.0 9.6 %copy-start.2 = (f32[256]{0:T(256)S(1)}, f32[256]{0:T(256)}, u32[]{:S(2)}) copy-start(f32[256]{0:T(256)} %param.14) | copy-start | bytes 3076
  0.0 9.6 %copy-start.1 = (f32[512]{0:T(512)S(1)}, f32[512]{0:T(512)}, u32[]{:S(2)}) copy-start(f32[512]{0:T(512)} %param.12) | copy-start | bytes 6148
  0.0 9.6 %copy-start = (f32[512]{0:T(512)S(1)}, f32[512]{0:T(512)}, u32[]{:S(2)}) copy-start(f32[512]{0:T(512)} %param.11) | copy-start | bytes 6148

commit v7 on v6

--- a/solution.py
+++ b/solution.py
@@ -12,7 +12,7 @@
 SEQ = 32
 TM = 4
 W = 32
-CHUNK = 16
+CHUNK = 32
 C1, C2, C3 = 512, 256, 128
 EPS = 1e-06
 
@@ -30,8 +30,7 @@
 
 def silu_normed(hidden, gain):
     factor = lax.rsqrt(jnp.mean(hidden * hidden, axis=1, keepdims=True) + EPS)
-    v = hidden * factor * gain
-    half = 0.5 * v
+    half = hidden * factor * (0.5 * gain)
     return (half + half * jnp.tanh(half)).astype(BF16)
 
 
@@ -90,25 +89,6 @@
     return values
 
 
-def add_taps(raw, summed, i, rows):
-    taps = {(j, k): raw[i, j, k, rows, :] for j in range(3) for k in range(3)}
-    values = merged(taps)
-    for n, p in enumerate(SUMS):
-        summed[i, n, rows, :] = values[p].astype(BF16)
-
-
-def tap_matrix(raw, summed, rp, b):
-    parts = []
-    for u in range(2):
-        for i in range(3):
-            if (rp, u, b) in RAW:
-                j, k = RAW[rp, u, b]
-                parts.append(raw[i, j, k])
-            else:
-                parts.append(summed[i, SUMS.index((rp, u, b))])
-    return jnp.concatenate(parts, axis=0)
-
-
 def add_timed_taps(raw, summed, rows, lanes):
     steps = [
         merged({(j, k): raw[i, j, k, rows, lanes] for j in range(3) for k in range(3)})
@@ -116,8 +96,8 @@
     ]
     for p in PLACES:
         g0, g1, g2 = (step[p] for step in steps)
-        outer, inner = 0.5 * (g0 + g2), 0.5 * g1
-        for n, value in enumerate((g0, outer + inner, outer - inner, g2)):
+        outer = g0 + g2
+        for n, value in enumerate((g0, outer + g1, outer - g1, g2)):
             if (n, p) in KEPT:
                 summed[KEPT.index((n, p)), rows, lanes] = value.astype(BF16)
 
@@ -218,10 +198,9 @@
 
     copy3.wait()
 
-    @pl.loop(0, C2 // 32)
+    @pl.loop(0, C2 // CHUNK)
     def _(n):
-        for i in range(3):
-            add_taps(w3, w3s, i, pl.ds(pl.multiple_of(32 * n, 32), 32))
+        add_timed_taps(w3, w3s, pl.ds(pl.multiple_of(CHUNK * n, CHUNK), CHUNK), pl.ds(0, C3))
 
     copy1.wait()
     for d in (0, 1, -1, 2, -2):
@@ -237,10 +216,17 @@
             all_of(d).wait_send()
 
 
-def convolutions(s, pat, w1, w2, w2s, b1_ref, g1_ref, b2_ref, g2_ref, x1, x2, first):
+def timed_terms(d):
+    half1, half2 = d[1] * 0.5, d[2] * 0.5
+    return d[0] - d[2], half1 + half2, half2 - half1, d[1] - d[3]
+
+
+def convolutions(
+    s, pat, w1, w2, w2s, w3, w3s, b1_ref, g1_ref, b2_ref, g2_ref, b3_ref, x1, x2, o32, first
+):
     start = 4 if first else 0
     size = W * (6 - start)
-    for r in range(3):
+    def first_hidden(r):
         q = jnp.clip(s - 1 + r, 0, SEQ - 1) - s + 1
         cols = []
         for i in range(3):
@@ -248,14 +234,17 @@
                 at = W * (i + start)
                 cols.append(pat[q + two, at : at + size, :].astype(BF16))
         lhs = jnp.concatenate(cols, axis=1)
-        hidden = jnp.dot(lhs, w1[...].reshape(768, C1), preferred_element_type=F32)
-        act = silu_normed(hidden + b1_ref[...], g1_ref[...])
+        return jnp.dot(lhs, w1[...].reshape(768, C1), preferred_element_type=F32)
+
+    hidden = [first_hidden(r) for r in range(3)]
+    for r in range(3):
+        act = silu_normed(hidden[r] + b1_ref[...], g1_ref[...])
         kinds = (1, 3) if first else (0, 1, 2, 3)
         d = {k: act[W * (k - start) : W * (k - start) + W] for k in range(start, 6)}
         for k in range(first, start):
             d[k] = d[start]
         for f in range(first, 4, 2):
-            terms = (d[f] - d[f + 2], d[f + 1] + d[f + 2], d[f + 2] - d[f + 1], d[f + 1] - d[f + 3])
+            terms = timed_terms([d[f + k] for k in range(4)])
             for n in kinds:
                 x1[n, r, W // 2 * f : W // 2 * f + W, :] = terms[n]
 
@@ -281,6 +270,7 @@
             return m[1], m[1] - m[3]
         return m[0] + (m[1] + m[2]), (m[1] - m[2]) - m[3]
 
+    acts = {}
     for rp in range(2):
         for later, (q0, qk, q2) in enumerate(zip(*[two_frames(rp, b) for b in range(3)])):
             qk = qk + b2_ref[...]
@@ -289,53 +279,36 @@
             for p, value in enumerate((even, odd)):
                 act = silu_normed(value, g2_ref[...])
                 for row in range(2):
-                    slot = 2 * row + 1 - rp
                     for f in range(first, 4, 2):
                         part = act[size * row + W // 2 * (f - first) :][:W]
-                        at = 64 * (f + later) + W * p
-                        x2[slot, at : at + W, :] = part
-
-
-def decode_kernel(
-    lat, w1, w2, w2s, w3, w3s, b1_ref, g1_ref, b2_ref, g2_ref, b3_ref,
-    out_ref,
-    pat, x1, x2, o32,
-):
-    s, t = lax.axis_index("seq"), lax.axis_index("tm")
-
-    patches(lat, pat, s, t)
-
-    @pl.when(t == 0)
-    def _():
-        convolutions(s, pat, w1, w2, w2s, b1_ref, g1_ref, b2_ref, g2_ref, x1, x2, 2)
-        for slot in range(4):
-            third = x2[slot, 128:192, :]
-            x2[slot, 0:64, :] = third
-            x2[slot, 64:128, :] = third
-
-    @pl.when(t > 0)
-    def _():
-        convolutions(s, pat, w1, w2, w2s, b1_ref, g1_ref, b2_ref, g2_ref, x1, x2, 0)
+                        acts[2 * row + 1 - rp, p, f + later] = part
+        for slot, p in [(2 * row + 1 - rp, p) for row in range(2) for p in range(2)]:
+            d = [acts[slot, p, f if f >= first else first] for f in range(4)]
+            terms = timed_terms(d)
+            for n in kinds:
+                x2[n, slot, W * p : W * p + W, :] = terms[n]
 
     slots = [jnp.where(s == 0, 1, 0), 1, 2, jnp.where(s == SEQ - 1, 2, 3)]
     col = lax.broadcasted_iota(jnp.int32, (32, 1), 0)
     for rp in range(2):
-        lhs = jnp.concatenate(
-            [
-                jnp.concatenate(
-                    [x2[slots[rp + u + row], 64 * i : 64 * i + 128, :] for row in range(2)],
-                    axis=0,
-                )
-                for u in range(2)
-                for i in range(3)
-            ],
-            axis=1,
-        )
-        rhs = jnp.concatenate([tap_matrix(w3, w3s, rp, b) for b in range(3)], axis=1)
-        res = jnp.dot(lhs, rhs, preferred_element_type=F32)
-        for row in range(2):
-            for f in range(2):
-                base = 128 * row + 64 * f
+        m = {}
+        for n in kinds:
+            lhs = jnp.concatenate(
+                [
+                    jnp.concatenate([x2[n, slots[rp + u + row]] for row in range(2)], axis=0)
+                    for u in range(2)
+                ],
+                axis=1,
+            )
+            taps = jnp.concatenate([timed_matrix(w3, w3s, rp, b, n) for b in range(3)], axis=1)
+            m[n] = jnp.dot(lhs, taps, preferred_element_type=F32)
+        if first:
+            frames = m[1], m[1] - m[3]
+        else:
+            frames = m[0] + (m[1] + m[2]), (m[1] - m[2]) - m[3]
+        for f, res in enumerate(frames):
+            for row in range(2):
+                base = 64 * row
                 (e0, ek, e2), (o0, ok, o2) = [
                     [
                         res[base + 32 * p : base + 32 * p + 32, C3 * b : C3 * b + C3]
@@ -353,6 +326,25 @@
                 )
                 for n, value in enumerate(values):
                     o32[f, 2 * row + rp, pl.ds(n, W, stride=4), :] = value
+
+def decode_kernel(
+    lat, w1, w2, w2s, w3, w3s, b1_ref, g1_ref, b2_ref, g2_ref, b3_ref,
+    out_ref,
+    pat, x1, x2, o32,
+):
+    s, t = lax.axis_index("seq"), lax.axis_index("tm")
+
+    patches(lat, pat, s, t)
+    refs = (pat, w1, w2, w2s, w3, w3s, b1_ref, g1_ref, b2_ref, g2_ref, b3_ref, x1, x2, o32)
+
+    @pl.when(t == 0)
+    def _():
+        convolutions(s, *refs, 2)
+
+    @pl.when(t > 0)
+    def _():
+        convolutions(s, *refs, 0)
+
     out_ref[...] = o32[...].astype(BF16)
 
 
@@ -369,7 +361,7 @@
             pltpu.VMEM((3, 3, 3, C1, C2), BF16),
             pltpu.VMEM((len(KEPT), C1, C2), BF16),
             pltpu.VMEM((3, 3, 3, C2, C3), BF16),
-            pltpu.VMEM((3, 8, C2, C3), BF16),
+            pltpu.VMEM((len(KEPT), C2, C3), BF16),
         ],
         in_specs=[hbm] * 4,
         out_specs=[vmem] * 6,
@@ -394,7 +386,7 @@
         scratch_shapes=[
             pltpu.VMEM((5, 8 * W, 128), F32),
             pltpu.VMEM((4, 3, 2 * W, C1), BF16),
-            pltpu.VMEM((4, 4 * 64, C2), BF16),
+            pltpu.VMEM((4, 4, 2 * W, C2), BF16),
             pltpu.VMEM((2, 4, 128, C3), F32),
         ],
         compiler_params=pltpu.CompilerParams(vmem_limit_bytes=24 << 20),

time: 15.3 us -> 14.8 us (0.967)
  Pallas kernels: 15 us -> 14.6 us
    pallas_call x1, Pallas kernels: 5.42 us -> 5.03 us  [per_device(): pl.pallas_call(decode_kernel, out_shape=jax.ShapeDtypeStruct((2, 4, 128,...]
where the time goes in v7:
time: 14.8 us; the launch traced here: 14.7 us
  Pallas kernels  14.6 us (99%)
    pallas_call x1, Pallas kernels, per_device(): pl.pallas_call(gather_kernel, out_shape=[pltpu.VMEM((5 * TM, 8, 128), BF1...  9.57 us
    pallas_call x1, Pallas kernels, per_device(): pl.pallas_call(decode_kernel, out_shape=jax.ShapeDtypeStruct((2, 4, 128,...  5.03 us

profile of v7, /device:TPU:15, one launch (start us, length us, event | category | flops | bytes accessed | tf_op | source)
XLA Modules:
  0.0 14.7 jit_solution(17928546770163898134)
XLA Ops:
  0.0 0.0 copy-start.4
  0.0 0.0 copy-start.3
  0.0 0.0 copy-start.2
  0.0 0.0 copy-start.1
  0.0 0.0 copy-start
  0.0 9.6 %gather.1 = (bf16[20,8,128]{2,1,0:T(8,128)(2,1)S(1)}, bf16[3,4,64,512]{3,2,1,0:T(8,128)(2,1)S(1)}, bf16[3,3,3,512,256]{4,3,2,1,0:T(8,128)(2,1)S(1)}, bf16[40,512...) custom-call(bf16[8,128]{1,0:T(8,128)(2,1)} %x_hbm.1, ...), custom_call_target="tpu_custom_call" | custom-call | tf_op jit(solution)/shard_map/gather/pallas_call | solution.py:356
  9.6 0.0 copy-done.4
  9.6 0.0 copy-done.3
  9.6 0.0 copy-done.2
  9.6 0.0 copy-done.1
  9.6 0.0 copy-done
  9.7 5.0 %decode.1 = bf16[2,4,128,128]{3,2,1,0:T(8,128)(2,1)} custom-call(bf16[20,8,128]{2,1,0:T(8,128)(2,1)S(1)} %get-tuple-element.11.lat, bf16[3,4,64,512]{3,2,1,0:T(8,128)(2,1)S(1)} %get-tuple-element.12.w1, bf16[3,3,3,512,256]{4,3,2,1,0:T(8,128)(2,1)S(1)} %get-tuple-element.13.w2, bf16[40,512,256]{2,1,0:T(8,128)(2,1)S(1)} %get-tuple-element.14.w2s, ...), custom_call_target="tpu_custom_call" | custom-call | tf_op jit(solution)/shard_map/decode/pallas_call | solution.py:381
Async XLA Ops:
  0.0 9.6 %copy-start.4 = (f32[128]{0:T(128)S(1)}, f32[128]{0:T(128)}, u32[]{:S(2)}) copy-start(f32[128]{0:T(128)} %param.17) | copy-start | bytes 1540
  0.0 9.6 %copy-start.3 = (f32[256]{0:T(256)S(1)}, f32[256]{0:T(256)}, u32[]{:S(2)}) copy-start(f32[256]{0:T(256)} %param.15) | copy-start | bytes 3076
  0.0 9.6 %copy-start.2 = (f32[256]{0:T(256)S(1)}, f32[256]{0:T(256)}, u32[]{:S(2)}) copy-start(f32[256]{0:T(256)} %param.14) | copy-start | bytes 3076
  0.0 9.6 %copy-start.1 = (f32[512]{0:T(512)S(1)}, f32[512]{0:T(512)}, u32[]{:S(2)}) copy-start(f32[512]{0:T(512)} %param.12) | copy-start | bytes 6148
  0.0 9.6 %copy-start = (f32[512]{0:T(512)S(1)}, f32[512]{0:T(512)}, u32[]{:S(2)}) copy-start(f32[512]{0:T(512)} %param.11) | copy-start | bytes 6148

commit v8 on v7

--- a/solution.py
+++ b/solution.py
@@ -89,7 +89,8 @@
     return values
 
 
-def add_timed_taps(raw, summed, rows, lanes):
+def add_timed_taps(raw, summed, rows, half):
+    lanes = pl.ds(128 * half, 128)
     steps = [
         merged({(j, k): raw[i, j, k, rows, lanes] for j in range(3) for k in range(3)})
         for i in range(3)
@@ -99,7 +100,7 @@
         outer = g0 + g2
         for n, value in enumerate((g0, outer + g1, outer - g1, g2)):
             if (n, p) in KEPT:
-                summed[KEPT.index((n, p)), rows, lanes] = value.astype(BF16)
+                summed[KEPT.index((n, p)), half, rows, :] = value.astype(BF16)
 
 
 def timed_matrix(raw, summed, rp, b, n):
@@ -107,7 +108,9 @@
     for u in range(2):
         p = (rp, u, b)
         if (n, p) in KEPT:
-            parts.append(summed[KEPT.index((n, p))])
+            kept = KEPT.index((n, p))
+            halves = [summed[kept, half] for half in range(summed.shape[1])]
+            parts.append(jnp.concatenate(halves, axis=1))
         else:
             j, k = RAW[p]
             parts.append(raw[0 if n == 0 else 2, j, k])
@@ -193,27 +196,27 @@
         @pl.loop(0, 128 // CHUNK)
         def _(n):
             rows = pl.ds(pl.multiple_of(128 * i + CHUNK * n, CHUNK), CHUNK)
-            for lane in range(0, C2, 128):
-                add_timed_taps(w2, w2s, rows, pl.ds(lane, 128))
+            for half in range(2):
+                add_timed_taps(w2, w2s, rows, half)
 
     copy3.wait()
 
     @pl.loop(0, C2 // CHUNK)
     def _(n):
-        add_timed_taps(w3, w3s, pl.ds(pl.multiple_of(CHUNK * n, CHUNK), CHUNK), pl.ds(0, C3))
+        add_timed_taps(w3, w3s, pl.ds(pl.multiple_of(CHUNK * n, CHUNK), CHUNK), 0)
 
     copy1.wait()
+    for d in (0, 1, -1, 2, -2):
+
+        @when_row(d)
+        def _():
+            all_of(d).wait_send()
+
     for d in (0, 1, -1, 2, -2):
 
         @when_row(d)
         def _():
             all_of(d).wait_recv()
-
-    for d in (0, 1, -1, 2, -2):
-
-        @when_row(d)
-        def _():
-            all_of(d).wait_send()
 
 
 def timed_terms(d):
@@ -359,9 +362,9 @@
             pltpu.VMEM((5 * TM, 8, 128), BF16),
             pltpu.VMEM((3, 4, 64, C1), BF16),
             pltpu.VMEM((3, 3, 3, C1, C2), BF16),
-            pltpu.VMEM((len(KEPT), C1, C2), BF16),
+            pltpu.VMEM((len(KEPT), 2, C1, 128), BF16),
             pltpu.VMEM((3, 3, 3, C2, C3), BF16),
-            pltpu.VMEM((len(KEPT), C2, C3), BF16),
+            pltpu.VMEM((len(KEPT), 1, C2, C3), BF16),
         ],
         in_specs=[hbm] * 4,
         out_specs=[vmem] * 6,

time: 14.8 us -> 14.7 us (level)
  no operation moved by 1% of the time
where the time goes in v8:
time: 14.7 us; the launch traced here: 14.6 us
  Pallas kernels  14.5 us (99%)
    pallas_call x1, Pallas kernels, per_device(): pl.pallas_call(gather_kernel, out_shape=[pltpu.VMEM((5 * TM, 8, 128), BF1...  9.56 us
    pallas_call x1, Pallas kernels, per_device(): pl.pallas_call(decode_kernel, out_shape=jax.ShapeDtypeStruct((2, 4, 128,...  4.95 us

profile of v8, /device:TPU:15, one launch (start us, length us, event | category | flops | bytes accessed | tf_op | source)
XLA Modules:
  0.0 14.6 jit_solution(14594835310243770486)
XLA Ops:
  0.0 0.0 copy-start.4
  0.0 0.0 copy-start.3
  0.0 0.0 copy-start.2
  0.0 0.0 copy-start.1
  0.0 0.0 copy-start
  0.0 9.6 %gather.1 = (bf16[20,8,128]{2,1,0:T(8,128)(2,1)S(1)}, bf16[3,4,64,512]{3,2,1,0:T(8,128)(2,1)S(1)}, bf16[3,3,3,512,256]{4,3,2,1,0:T(8,128)(2,1)S(1)}, bf16[40,2,5...) custom-call(bf16[8,128]{1,0:T(8,128)(2,1)} %x_hbm.1, ...), custom_call_target="tpu_custom_call" | custom-call | tf_op jit(solution)/shard_map/gather/pallas_call | solution.py:359
  9.6 0.0 copy-done.4
  9.6 0.0 copy-done.3
  9.6 0.0 copy-done.2
  9.6 0.0 copy-done.1
  9.6 0.0 copy-done
  9.6 5.0 %decode.1 = bf16[2,4,128,128]{3,2,1,0:T(8,128)(2,1)} custom-call(bf16[20,8,128]{2,1,0:T(8,128)(2,1)S(1)} %get-tuple-element.11.lat, bf16[3,4,64,512]{3,2,1,0:T(8,128)(2,1)S(1)} %get-tuple-element.12.w1, bf16[3,3,3,512,256]{4,3,2,1,0:T(8,128)(2,1)S(1)} %get-tuple-element.13.w2, bf16[40,2,512,128]{3,2,1,0:T(8,128)(2,1)S(1)} %get-tuple-element.14.w2s, ...), custom_call_target="tpu_custom_call" | custom-call | tf_op jit(solution)/shard_map/decode/pallas_call | solution.py:384
Async XLA Ops:
  0.0 9.6 %copy-start.4 = (f32[128]{0:T(128)S(1)}, f32[128]{0:T(128)}, u32[]{:S(2)}) copy-start(f32[128]{0:T(128)} %param.17) | copy-start | bytes 1540
  0.0 9.6 %copy-start.3 = (f32[256]{0:T(256)S(1)}, f32[256]{0:T(256)}, u32[]{:S(2)}) copy-start(f32[256]{0:T(256)} %param.15) | copy-start | bytes 3076
  0.0 9.6 %copy-start.2 = (f32[256]{0:T(256)S(1)}, f32[256]{0:T(256)}, u32[]{:S(2)}) copy-start(f32[256]{0:T(256)} %param.14) | copy-start | bytes 3076
  0.0 9.6 %copy-start.1 = (f32[512]{0:T(512)S(1)}, f32[512]{0:T(512)}, u32[]{:S(2)}) copy-start(f32[512]{0:T(512)} %param.12) | copy-start | bytes 6148
  0.0 9.6 %copy-start = (f32[512]{0:T(512)S(1)}, f32[512]{0:T(512)}, u32[]{:S(2)}) copy-start(f32[512]{0:T(512)} %param.11) | copy-start | bytes 6148

commit v9 on v8

--- a/solution.py
+++ b/solution.py
@@ -225,24 +225,30 @@
 
 
 def convolutions(
-    s, pat, w1, w2, w2s, w3, w3s, b1_ref, g1_ref, b2_ref, g2_ref, b3_ref, x1, x2, o32, first
+    s, t, lat, out_ref, pat, w1, w2, w2s, w3, w3s, b1_ref, g1_ref, b2_ref, g2_ref, b3_ref, x1, x2, o32, first
 ):
+    patches(lat, pat, s, t)
     start = 4 if first else 0
     size = W * (6 - start)
     def first_hidden(r):
-        q = jnp.clip(s - 1 + r, 0, SEQ - 1) - s + 1
         cols = []
         for i in range(3):
             for two in (0, 2):
                 at = W * (i + start)
-                cols.append(pat[q + two, at : at + size, :].astype(BF16))
+                cols.append(pat[r + two, at : at + size, :].astype(BF16))
         lhs = jnp.concatenate(cols, axis=1)
         return jnp.dot(lhs, w1[...].reshape(768, C1), preferred_element_type=F32)
 
-    hidden = [first_hidden(r) for r in range(3)]
-    for r in range(3):
+    kinds = (1, 3) if first else (0, 1, 2, 3)
+    hidden = {r: first_hidden(r) for r in (1, 0, 2)}
+    acts = {}
+    for r in (1, 0, 2):
         act = silu_normed(hidden[r] + b1_ref[...], g1_ref[...])
-        kinds = (1, 3) if first else (0, 1, 2, 3)
+        if r == 0:
+            act = jnp.where(s == 0, acts[1], act)
+        if r == 2:
+            act = jnp.where(s == SEQ - 1, acts[1], act)
+        acts[r] = act
         d = {k: act[W * (k - start) : W * (k - start) + W] for k in range(start, 6)}
         for k in range(first, start):
             d[k] = d[start]
@@ -291,14 +297,21 @@
             for n in kinds:
                 x2[n, slot, W * p : W * p + W, :] = terms[n]
 
-    slots = [jnp.where(s == 0, 1, 0), 1, 2, jnp.where(s == SEQ - 1, 2, 3)]
+    def row_terms(n, slot):
+        value = x2[n, slot]
+        if slot == 0:
+            value = jnp.where(s == 0, x2[n, 1], value)
+        if slot == 3:
+            value = jnp.where(s == SEQ - 1, x2[n, 2], value)
+        return value
+
     col = lax.broadcasted_iota(jnp.int32, (32, 1), 0)
     for rp in range(2):
         m = {}
         for n in kinds:
             lhs = jnp.concatenate(
                 [
-                    jnp.concatenate([x2[n, slots[rp + u + row]] for row in range(2)], axis=0)
+                    jnp.concatenate([row_terms(n, rp + u + row) for row in range(2)], axis=0)
                     for u in range(2)
                 ],
                 axis=1,
@@ -329,6 +342,7 @@
                 )
                 for n, value in enumerate(values):
                     o32[f, 2 * row + rp, pl.ds(n, W, stride=4), :] = value
+                out_ref[f, 2 * row + rp] = o32[f, 2 * row + rp].astype(BF16)
 
 def decode_kernel(
     lat, w1, w2, w2s, w3, w3s, b1_ref, g1_ref, b2_ref, g2_ref, b3_ref,
@@ -337,18 +351,15 @@
 ):
     s, t = lax.axis_index("seq"), lax.axis_index("tm")
 
-    patches(lat, pat, s, t)
-    refs = (pat, w1, w2, w2s, w3, w3s, b1_ref, g1_ref, b2_ref, g2_ref, b3_ref, x1, x2, o32)
+    refs = (lat, out_ref, pat, w1, w2, w2s, w3, w3s, b1_ref, g1_ref, b2_ref, g2_ref, b3_ref, x1, x2, o32)
 
     @pl.when(t == 0)
     def _():
-        convolutions(s, *refs, 2)
+        convolutions(s, t, *refs, 2)
 
     @pl.when(t > 0)
     def _():
-        convolutions(s, *refs, 0)
-
-    out_ref[...] = o32[...].astype(BF16)
+        convolutions(s, t, *refs, 0)
 
 
 def per_device(latent, w1, b1, g1, w2, b2, g2, w3, b3):

time: 14.7 us -> 14.6 us (level)
  no operation moved by 1% of the time
where the time goes in v9:
time: 14.6 us; the launch traced here: 14.5 us
  Pallas kernels  14.4 us (99%)
    pallas_call x1, Pallas kernels, per_device(): pl.pallas_call(gather_kernel, out_shape=[pltpu.VMEM((5 * TM, 8, 128), BF1...  9.56 us
    pallas_call x1, Pallas kernels, per_device(): pl.pallas_call(decode_kernel, out_shape=jax.ShapeDtypeStruct((2, 4, 128,...  4.89 us

profile of v9, /device:TPU:15, one launch (start us, length us, event | category | flops | bytes accessed | tf_op | source)
XLA Modules:
  0.0 14.5 jit_solution(7227394771497330993)
XLA Ops:
  0.0 0.0 copy-start.4
  0.0 0.0 copy-start.3
  0.0 0.0 copy-start.2
  0.0 0.0 copy-start.1
  0.0 0.0 copy-start
  0.0 9.6 %gather.1 = (bf16[20,8,128]{2,1,0:T(8,128)(2,1)S(1)}, bf16[3,4,64,512]{3,2,1,0:T(8,128)(2,1)S(1)}, bf16[3,3,3,512,256]{4,3,2,1,0:T(8,128)(2,1)S(1)}, bf16[40,2,5...) custom-call(bf16[8,128]{1,0:T(8,128)(2,1)} %x_hbm.1, ...), custom_call_target="tpu_custom_call" | custom-call | tf_op jit(solution)/shard_map/gather/pallas_call | solution.py:370
  9.6 0.0 copy-done.4
  9.6 0.0 copy-done.3
  9.6 0.0 copy-done.2
  9.6 0.0 copy-done.1
  9.6 0.0 copy-done
  9.6 4.9 %decode.1 = bf16[2,4,128,128]{3,2,1,0:T(8,128)(2,1)} custom-call(bf16[20,8,128]{2,1,0:T(8,128)(2,1)S(1)} %get-tuple-element.11.lat, bf16[3,4,64,512]{3,2,1,0:T(8,128)(2,1)S(1)} %get-tuple-element.12.w1, bf16[3,3,3,512,256]{4,3,2,1,0:T(8,128)(2,1)S(1)} %get-tuple-element.13.w2, bf16[40,2,512,128]{3,2,1,0:T(8,128)(2,1)S(1)} %get-tuple-element.14.w2s, ...), custom_call_target="tpu_custom_call" | custom-call | tf_op jit(solution)/shard_map/decode/pallas_call | solution.py:395
Async XLA Ops:
  0.0 9.6 %copy-start.4 = (f32[128]{0:T(128)S(1)}, f32[128]{0:T(128)}, u32[]{:S(2)}) copy-start(f32[128]{0:T(128)} %param.17) | copy-start | bytes 1540
  0.0 9.6 %copy-start.3 = (f32[256]{0:T(256)S(1)}, f32[256]{0:T(256)}, u32[]{:S(2)}) copy-start(f32[256]{0:T(256)} %param.15) | copy-start | bytes 3076
  0.0 9.6 %copy-start.2 = (f32[256]{0:T(256)S(1)}, f32[256]{0:T(256)}, u32[]{:S(2)}) copy-start(f32[256]{0:T(256)} %param.14) | copy-start | bytes 3076
  0.0 9.6 %copy-start.1 = (f32[512]{0:T(512)S(1)}, f32[512]{0:T(512)}, u32[]{:S(2)}) copy-start(f32[512]{0:T(512)} %param.12) | copy-start | bytes 6148
  0.0 9.6 %copy-start = (f32[512]{0:T(512)S(1)}, f32[512]{0:T(512)}, u32[]{:S(2)}) copy-start(f32[512]{0:T(512)} %param.11) | copy-start | bytes 6148
